TPU v7x, 128 devices: a whole 4x4x4 slice. The times are simulated.
128 devices in a mesh: dp: 4 (over y), expert: 32 (over z, x, core).
Axes of the slice: x: 4, y: 4, z: 4, core: 2. Of those that a mesh axis runs over, the one named last changes fastest.
Arguments:
- tokens: bfloat16 [16384, 4096], P(('dp', 'expert')), may hold values from -6 to 6
- out_grad: bfloat16 [16384, 4096], P(('dp', 'expert')), may hold values from -6 to 6
- route_slots: int32 [4, 32, 32, 16], P('dp', 'expert'), may hold values from -1 to 127, as said below
- expert_counts: int32 [16384], P(('dp', 'expert')), may hold values from 0 to 32, as said below
- router_weight: float32 [4096, 32], replicated, may hold values from -0.09375 to 0.09375
- up_weight: bfloat16 [32, 4096, 1024], P('expert'), may hold values from -0.09375 to 0.09375
- down_weight: bfloat16 [32, 4096, 1024], P('expert'), may hold values from -0.1875 to 0.1875
Outputs:
- tokens_grad: bfloat16 [16384, 4096], P(('dp', 'expert'))
- up_grad: bfloat16 [32, 4096, 1024], P('expert', 'dp')
- down_grad: bfloat16 [32, 4096, 1024], P('expert', 'dp')
- router_grad: float32 [4096, 32], P(None, 'expert')
Inputs may be any that keep to these rules, and one draw needn't show every extreme that they name: In route_slots[p, s, e, :] the chosen local tokens are distinct and come first, then -1; every list holds at least one token. In every batch shard some expert takes 16 tokens from every device of it. On every device one local token is chosen by every expert. expert_counts of a token equals the number of lists of route_slots that hold it.
All inputs are finite; a program needn't handle non-finite values.
Results may differ from a plain program's by a relative error of at most 0.017.
Values may be sent and summed in bfloat16 or wider, within the bound.
A program may use at most 192 MiB of HBM per device.

v0:
```python
import jax
import jax.numpy as jnp
from jax import lax
from jax.sharding import PartitionSpec as P


def gelu_pair(values):
    inner = 0.7978845608 * (values + 0.044715 * values * values * values)
    tangent = jnp.tanh(inner)
    result = 0.5 * values * (1.0 + tangent)
    slope = 0.5 * (1.0 + tangent) + 0.5 * values * (1.0 - tangent * tangent) * 0.7978845608 * (
        1.0 + 3.0 * 0.044715 * values * values
    )
    return (result, slope)


def on_device(tokens, out_grad, route_slots, expert_counts, router_weight, up_weight, down_weight):
    experts = lax.axis_size("expert")
    tok_rows = tokens.shape[0]
    width = tokens.shape[1]
    slots = route_slots[0, 0]
    per_slot = slots.shape[1]
    received = experts * per_slot
    contract = (((0,), (0,)), ((), ()))
    trailing = (((1,), (1,)), ((), ()))
    highest = lax.Precision.HIGHEST
    valid = slots >= 0
    picks = slots[:, :, None] == jnp.arange(tok_rows, dtype=jnp.int32)[None, None, :]
    pick_float = picks.astype(jnp.float32)
    pick_half = picks.astype(jnp.bfloat16).reshape(received, tok_rows)
    logits = jnp.dot(tokens.astype(jnp.float32), router_weight, precision=highest)
    gates = jax.nn.sigmoid(logits)
    gate_slot = jnp.einsum("est,te->es", pick_float, gates, precision=highest)
    count_slot = jnp.einsum(
        "est,t->es", pick_float, expert_counts.astype(jnp.float32), precision=highest
    )
    safe_count = jnp.where(valid, count_slot, 1.0)
    weight_slot = jnp.where(valid, gate_slot / safe_count, 0.0)
    slope_slot = jnp.where(valid, gate_slot * (1.0 - gate_slot) / safe_count, 0.0)
    send_rows = (
        jnp.dot(pick_half, tokens, preferred_element_type=jnp.float32)
        .astype(jnp.bfloat16)
        .reshape(experts, per_slot, width)
    )
    send_grads = (
        jnp.dot(pick_half, out_grad, preferred_element_type=jnp.float32)
        .astype(jnp.bfloat16)
        .reshape(experts, per_slot, width)
    )
    coefs = weight_slot[:, None, :]
    got_rows, got_grads, got_coefs = (
        lax.all_to_all(send_rows, "expert", split_axis=0, concat_axis=0, tiled=True),
        lax.all_to_all(send_grads, "expert", split_axis=0, concat_axis=0, tiled=True),
        lax.all_to_all(
            coefs.astype(jnp.bfloat16), "expert", split_axis=0, concat_axis=0, tiled=True
        ).astype(coefs.dtype),
    )
    rows_in = got_rows.reshape(received, width)
    grads_in = got_grads.reshape(received, width)
    weight_in = got_coefs[:, 0, :].reshape(received)
    w_up = up_weight[0]
    w_down = down_weight[0]
    pre = jnp.dot(rows_in, w_up, preferred_element_type=jnp.float32)
    active, slope = gelu_pair(pre)
    active = active.astype(jnp.bfloat16)
    output = lax.dot_general(active, w_down, trailing, preferred_element_type=jnp.float32)
    grads_float = grads_in.astype(jnp.float32)
    score = jnp.sum(grads_float * output, axis=1)
    out_scaled = (weight_in[:, None] * grads_float).astype(jnp.bfloat16)
    act_grad = jnp.dot(out_scaled, w_down, preferred_element_type=jnp.float32)
    pre_grad = (act_grad * slope).astype(jnp.bfloat16)
    row_grad = lax.dot_general(pre_grad, w_up, trailing, preferred_element_type=jnp.float32).astype(
        jnp.bfloat16
    )
    back_rows, back_score = (
        lax.all_to_all(
            row_grad.reshape(experts, per_slot, width),
            "expert",
            split_axis=0,
            concat_axis=0,
            tiled=True,
        ),
        lax.all_to_all(
            score.reshape(experts, per_slot).astype(jnp.bfloat16),
            "expert",
            split_axis=0,
            concat_axis=0,
            tiled=True,
        ).astype(jnp.float32),
    )
    up_sum = lax.psum_scatter(
        lax.dot_general(rows_in, pre_grad, contract, preferred_element_type=jnp.float32).astype(
            jnp.bfloat16
        ),
        "dp",
        scatter_dimension=0,
        tiled=True,
    )
    down_sum = lax.psum_scatter(
        lax.dot_general(out_scaled, active, contract, preferred_element_type=jnp.float32).astype(
            jnp.bfloat16
        ),
        "dp",
        scatter_dimension=0,
        tiled=True,
    )
    moe_grad = lax.dot_general(
        pick_half, back_rows.reshape(received, width), contract, preferred_element_type=jnp.float32
    )
    logit_grad = jnp.einsum("est,es->te", pick_float, back_score * slope_slot, precision=highest)
    tokens_grad = (moe_grad + jnp.dot(logit_grad, router_weight.T, precision=highest)).astype(
        jnp.bfloat16
    )
    local_terms = jnp.dot(tokens.astype(jnp.float32).T, logit_grad, precision=highest)
    own_column = lax.psum_scatter(
        local_terms.astype(jnp.bfloat16), "expert", scatter_dimension=1, tiled=True
    ).astype(jnp.float32)
    router_grad = lax.psum(own_column, "dp")
    return (tokens_grad, up_sum[None], down_sum[None], router_grad)


def solution(mesh):
    return jax.shard_map(
        on_device,
        mesh=mesh,
        in_specs=(
            P(("dp", "expert"), None),
            P(("dp", "expert"), None),
            P("dp", "expert", None, None),
            P(("dp", "expert")),
            P(),
            P("expert", None, None),
            P("expert", None, None),
        ),
        out_specs=(
            P(("dp", "expert"), None),
            P("expert", "dp", None),
            P("expert", "dp", None),
            P(None, "expert"),
        ),
        check_vma=False,
    )
```

profile of v0, /device:TPU:1, one launch (start us, length us, event | category | flops | bytes accessed | tf_op | source)
XLA Modules:
  0.0 347.9 jit_solution(6306179200393254704)
XLA Ops:
  8.0 0.0 copy-start
  8.0 0.9 copy.24
  8.9 0.1 eq.28
  9.0 0.3 copy-done
  9.2 3.2 convolution_convert_fusion.2
  12.5 0.0 copy-start.3
  12.5 9.6 %all-to-all-start.2 = ((bf16[32,16,4096]{2,1,0:T(8,128)(2,1)}), bf16[32,16,4096]{2,1,0:T(8,128)(2,1)}, u32[]{:S(2)}, u32[]{:S(2)}) async-start(bf16[32,16,4096]{2,1,0:T(8,128)(2,1)} %bitcast.85), calls=%async_computation.2 | async-start | bytes 8388608 | tf_op jit(solution)/shard_map/all_to_all | solution.py:52
  22.1 0.0 copy-done.3
  22.1 3.3 convolution_convert_fusion.3
  25.4 47.0 %all-to-all-done.2 = bf16[32,16,4096]{2,1,0:T(8,128)(2,1)} async-done(((bf16[32,16,4096]{2,1,0:T(8,128)(2,1)}), bf16[32,16,4096]{2,1,0:T(8,128)(2,1)}, u32[]{:S(2)}, u32[]{:S(2)}) %all-to-all-start.2) | async-done | bytes 4194336 | tf_op jit(solution)/shard_map/all_to_all | solution.py:52
  72.4 0.0 copy-start.4
  72.4 0.0 copy-start.2
  72.4 8.1 %all-to-all-start.1 = ((bf16[32,16,4096]{2,1,0:T(8,128)(2,1)}), bf16[32,16,4096]{2,1,0:T(8,128)(2,1)}, u32[]{:S(2)}, u32[]{:S(2)}) async-start(bf16[32,16,4096]{2,1,0:T(8,128)(2,1)} %bitcast.84), calls=%async_computation.1 | async-start | bytes 8388608 | tf_op jit(solution)/shard_map/all_to_all | solution.py:53
  80.5 0.0 copy-done.4
  80.5 0.1 iota_compare_fusion.3
  80.6 0.0 copy-done.2
  80.7 1.1 fusion.30
  81.8 0.3 fusion.33
  82.1 10.5 %fusion.5 = f32[512,1024]{1,0:T(8,128)} fusion(bf16[512,4096]{1,0:T(8,128)(2,1)} %bitcast.12, bf16[1,4096,1024]{2,1,0:T(8,128)(2,1)} %param.12), kind=kOutput, calls=%fused_computation.8 | convolution fusion | flops 4294967296 | bytes 14680064 | tf_op jit(solution)/shard_map/dot_general | solution.py:63
  92.6 0.0 copy-start.5
  92.6 38.3 %all-to-all-done.1 = bf16[32,16,4096]{2,1,0:T(8,128)(2,1)} async-done(((bf16[32,16,4096]{2,1,0:T(8,128)(2,1)}), bf16[32,16,4096]{2,1,0:T(8,128)(2,1)}, u32[]{:S(2)}, u32[]{:S(2)}) %all-to-all-start.1) | async-done | bytes 4194336 | tf_op jit(solution)/shard_map/all_to_all | solution.py:53
  130.9 10.0 %fusion.1 = bf16[512]{0:T(512)(128)(2,1)S(1)} fusion(bf16[32,16,4096]{2,1,0:T(8,128)(2,1)} %all-to-all-done.1, bf16[1,4096,1024]{2,1,0:T(8,128)(2,1)} %param.13, f32[512,1024]{1,0:T(8,128)} %fusion.5), kind=kOutput, calls=%fused_computation.4 | convolution fusion | flops 4305976832 | bytes 14681088 | tf_op jit(solution)/shard_map/dot_general | solution.py:66
  140.8 0.7 convert_element_type.112
  141.5 7.0 %all-to-all-start.4 = ((bf16[32,1,16]{2,1,0:T(2,128)(2,1)}), bf16[32,1,16]{2,1,0:T(2,128)(2,1)S(1)}, u32[]{:S(2)}, u32[]{:S(2)}) async-start(bf16[32,1,16]{2,1,0:T(2,128)(2,1)} %convert_element_type.112), calls=%async_computation.4 | async-start | bytes 32768 | tf_op jit(solution)/shard_map/all_to_all | solution.py:83
  148.6 0.0 copy-done.5
  148.6 0.7 fusion.35
  149.2 0.1 copy.30
  149.3 6.2 %all-to-all-done.4 = bf16[32,1,16]{2,1,0:T(2,128)(2,1)S(1)} async-done(((bf16[32,1,16]{2,1,0:T(2,128)(2,1)}), bf16[32,1,16]{2,1,0:T(2,128)(2,1)S(1)}, u32[]{:S(2)}, u32[]{:S(2)}) %all-to-all-start.4) | async-done | bytes 1056 | tf_op jit(solution)/shard_map/all_to_all | solution.py:83
  155.5 0.1 copy.27
  155.7 0.1 copy.32
  155.7 0.3 fusion.31
  156.0 0.7 copy.23
  156.7 4.1 %all-to-all-start = ((bf16[32,1,16]{2,1,0:T(2,128)(2,1)}), bf16[32,1,16]{2,1,0:T(2,128)(2,1)S(1)}, u32[]{:S(2)}, u32[]{:S(2)}) async-start(bf16[32,1,16]{2,1,0:T(2,128)(2,1)} %copy.23), calls=%async_computation | async-start | bytes 32768 | tf_op jit(solution)/shard_map/all_to_all | solution.py:54
  160.8 0.0 all-reduce.3.cloned.1.call-start
  160.9 1.2 fusion.15
  162.1 0.0 all-reduce.3.cloned.1.call-update
  162.1 0.0 reduce-scatter.5.cloned.1.call-start
  162.2 5.6 %all-to-all-done = bf16[32,1,16]{2,1,0:T(2,128)(2,1)S(1)} async-done(((bf16[32,1,16]{2,1,0:T(2,128)(2,1)}), bf16[32,1,16]{2,1,0:T(2,128)(2,1)S(1)}, u32[]{:S(2)}, u32[]{:S(2)}) %all-to-all-start) | async-done | bytes 1056 | tf_op jit(solution)/shard_map/all_to_all | solution.py:54
  167.8 0.1 convert_reduce_fusion
  167.9 0.1 mul.97
  167.9 0.0 copy-start.7
  167.9 3.7 %fusion.2 = bf16[512,4096]{1,0:T(8,128)(2,1)S(1)} fusion(bf16[32,16,4096]{2,1,0:T(8,128)(2,1)} %all-to-all-done.1, f32[512]{0:T(512)S(1)} %mul.97), kind=kLoop, calls=%fused_computation.5 | loop fusion | flops 6291456 | bytes 8390656 | tf_op jit(solution)/shard_map/convert_element_type | solution.py:69
  171.6 0.0 copy-done.7
  171.6 7.2 %convolution_convert_fusion = bf16[4096,1024]{1,0:T(8,128)(2,1)} fusion(bf16[512,4096]{1,0:T(8,128)(2,1)S(1)} %fusion.2, f32[512,1024]{1,0:T(8,128)S(1)} %copy-done.7), kind=kOutput, calls=%fused_computation.14 | convolution fusion | flops 4303880192 | bytes 14680064 | tf_op jit(solution)/shard_map/dot_general | solution.py:100
  178.8 0.0 reduce-scatter.5.cloned.1.call-update
  178.9 0.0 reduce-scatter.3.cloned.1.call-start
  178.9 0.0 copy-start.8
  179.0 3.9 %fusion = bf16[32,16,4096]{2,1,0:T(8,128)(2,1)S(1)} fusion(bf16[32,16,4096]{2,1,0:T(8,128)(2,1)} %all-to-all-done.1, f32[32,16]{1,0:T(8,128)S(1)} %bitcast.91), kind=kLoop, calls=%fused_computation.3 | loop fusion | flops 6291456 | bytes 8390656 | tf_op jit(solution)/shard_map/convert_element_type | solution.py:69
  182.8 0.0 copy-done.8
  182.9 9.4 %fusion.25 = bf16[512,1024]{1,0:T(8,128)(2,1)S(1)} fusion(f32[512,1024]{1,0:T(8,128)S(1)} %copy-done.8, bf16[512,4096]{1,0:T(8,128)(2,1)S(1)} %bitcast.87, bf16[1,4096,1024]{2,1,0:T(8,128)(2,1)} %param.13), kind=kOutput, calls=%fused_computation.33 | convolution fusion | flops 4304928768 | bytes 15728640 | tf_op jit(solution)/shard_map/dot_general | solution.py:70
  192.3 9.0 %convolution_convert_fusion.1 = bf16[4096,1024]{1,0:T(8,128)(2,1)} fusion(bf16[512,4096]{1,0:T(8,128)(2,1)} %bitcast.12, bf16[512,1024]{1,0:T(8,128)(2,1)S(1)} %fusion.25), kind=kOutput, calls=%fused_computation.15 | convolution fusion | flops 4299161600 | bytes 13631488 | tf_op jit(solution)/shard_map/dot_general | solution.py:92
  201.3 0.0 reduce-scatter.3.cloned.1.call-update
  201.4 9.6 %fusion.11 = bf16[512,4096]{1,0:T(8,128)(2,1)} fusion(bf16[512,1024]{1,0:T(8,128)(2,1)S(1)} %fusion.25, bf16[1,4096,1024]{2,1,0:T(8,128)(2,1)} %param.12), kind=kOutput, calls=%fused_computation.16 | convolution fusion | flops 4297064448 | bytes 13631488 | tf_op jit(solution)/shard_map/dot_general | solution.py:72
  211.0 5.4 %all-to-all-start.3 = ((bf16[32,16,4096]{2,1,0:T(8,128)(2,1)}), bf16[32,16,4096]{2,1,0:T(8,128)(2,1)}, u32[]{:S(2)}, u32[]{:S(2)}) async-start(bf16[32,16,4096]{2,1,0:T(8,128)(2,1)} %bitcast.86), calls=%async_computation.3 | async-start | bytes 8388608 | tf_op jit(solution)/shard_map/all_to_all | solution.py:76
  216.4 0.0 copy-done.6
  216.4 0.6 dynamic-slice
  217.0 76.9 %all-reduce.3.cloned.1.call-done = bf16[4096,32]{0,1:T(8,128)(2,1)} async-done(((bf16[4096,32]{0,1:T(8,128)(2,1)}), bf16[4096,32]{0,1:T(8,128)(2,1)}) %all-reduce.3.cloned.1.call-update) | async-done | bytes 262160
  293.8 1.5 dynamic-slice_convert_fusion
  295.3 16.0 %psum.7 = f32[4096,1]{0,1:T(1,128)} all-reduce(f32[4096,1]{0,1:T(1,128)S(1)} %dynamic-slice_convert_fusion), channel_id=1, replica_groups=mesh['dp'=4,'expert'=32] {'dp'}, use_global_device_ids=true, to_apply=%region_4.5 | all-reduce | flops 4096 | bytes 32768 | tf_op jit(solution)/shard_map/psum | solution.py:118
  311.3 0.0 all-to-all-done.3
  311.3 5.0 %convolution_bitcast_fusion = f32[128,4096]{1,0:T(8,128)S(1)} fusion(bf16[32,16,4096]{2,1,0:T(8,128)(2,1)} %all-to-all-done.3, s32[32,16]{0,1:T(8,128)S(1)} %bitcast.90), kind=kOutput, calls=%fused_computation.20 | convolution fusion | flops 536936448 | bytes 6293504 | tf_op jit(solution)/shard_map/dot_general | solution.py:107
  316.3 2.8 fusion.14
  319.1 21.4 %reduce-scatter.3.cloned.1.call-done = bf16[1024,1024]{1,0:T(8,128)(2,1)} async-done(((bf16[4096,1024]{1,0:T(8,128)(2,1)}), bf16[1024,1024]{1,0:T(8,128)(2,1)}) %reduce-scatter.3.cloned.1.call-update) | async-done | bytes 2097168 | tf_op jit(solution)/shard_map/reduce_scatter | solution.py:91
  340.5 0.0 copy-done.1
  (6 shorter events, 0.0 us)
Async XLA Ops:
  8.0 1.2 copy-start
  12.5 9.6 %copy-start.3 = (bf16[128,4096]{1,0:T(8,128)(2,1)S(1)}, bf16[128,4096]{1,0:T(8,128)(2,1)}, u32[]{:S(2)}) copy-start(bf16[128,4096]{1,0:T(8,128)(2,1)} %param.8) | copy-start | bytes 3145732
  12.5 59.9 %all-to-all-start.2 = ((bf16[32,16,4096]{2,1,0:T(8,128)(2,1)}), bf16[32,16,4096]{2,1,0:T(8,128)(2,1)}, u32[]{:S(2)}, u32[]{:S(2)}) async-start(bf16[32,16,4096]{2,1,0:T(8,128)(2,1)} %bitcast.85), calls=%async_computation.2 | async-start | bytes 8388608 | tf_op jit(solution)/shard_map/all_to_all | solution.py:52
  72.4 8.1 %copy-start.4 = (s32[1,1,32,16]{2,3,1,0:T(8,128)S(1)}, s32[1,1,32,16]{2,3,1,0:T(8,128)}, u32[]{:S(2)}) copy-start(s32[1,1,32,16]{2,3,1,0:T(8,128)} %param.9) | copy-start | bytes 6148
  72.4 8.3 %copy-start.2 = (f32[4096,32]{0,1:T(8,128)S(1)}, f32[4096,32]{0,1:T(8,128)}, u32[]{:S(2)}) copy-start(f32[4096,32]{0,1:T(8,128)} %param.11) | copy-start | bytes 1572868
  72.4 58.5 %all-to-all-start.1 = ((bf16[32,16,4096]{2,1,0:T(8,128)(2,1)}), bf16[32,16,4096]{2,1,0:T(8,128)(2,1)}, u32[]{:S(2)}, u32[]{:S(2)}) async-start(bf16[32,16,4096]{2,1,0:T(8,128)(2,1)} %bitcast.84), calls=%async_computation.1 | async-start | bytes 8388608 | tf_op jit(solution)/shard_map/all_to_all | solution.py:53
  92.6 56.0 %copy-start.5 = (s32[128]{0:T(128)S(1)}, s32[128]{0:T(128)}, u32[]{:S(2)}) copy-start(s32[128]{0:T(128)} %param.10) | copy-start | bytes 1540
  141.5 14.0 %all-to-all-start.4 = ((bf16[32,1,16]{2,1,0:T(2,128)(2,1)}), bf16[32,1,16]{2,1,0:T(2,128)(2,1)S(1)}, u32[]{:S(2)}, u32[]{:S(2)}) async-start(bf16[32,1,16]{2,1,0:T(2,128)(2,1)} %convert_element_type.112), calls=%async_computation.4 | async-start | bytes 32768 | tf_op jit(solution)/shard_map/all_to_all | solution.py:83
  156.7 11.1 %all-to-all-start = ((bf16[32,1,16]{2,1,0:T(2,128)(2,1)}), bf16[32,1,16]{2,1,0:T(2,128)(2,1)S(1)}, u32[]{:S(2)}, u32[]{:S(2)}) async-start(bf16[32,1,16]{2,1,0:T(2,128)(2,1)} %copy.23), calls=%async_computation | async-start | bytes 32768 | tf_op jit(solution)/shard_map/all_to_all | solution.py:54
  160.8 133.0 %all-reduce.3.cloned.1.call-start = ((), (), s32[]{:S(2)}) async-start(), calls=%async_computation.9 | async-start | bytes 524288
  162.1 157.0 %reduce-scatter.5.cloned.1.call-start = ((), (), s32[]{:S(2)}) async-start(), calls=%async_computation.8 | async-start | bytes 10485760 | tf_op jit(solution)/shard_map/reduce_scatter | solution.py:99
  167.9 3.7 %copy-start.7 = (f32[512,1024]{1,0:T(8,128)S(1)}, f32[512,1024]{1,0:T(8,128)}, u32[]{:S(2)}) copy-start(f32[512,1024]{1,0:T(8,128)} %fusion.5) | copy-start | bytes 6291460
  178.9 161.6 %reduce-scatter.3.cloned.1.call-start = ((), (), s32[]{:S(2)}) async-start(), calls=%async_computation.7 | async-start | bytes 10485760 | tf_op jit(solution)/shard_map/reduce_scatter | solution.py:91
  178.9 3.9 %copy-start.8 = (f32[512,1024]{1,0:T(8,128)S(1)}, f32[512,1024]{1,0:T(8,128)}, u32[]{:S(2)}) copy-start(f32[512,1024]{1,0:T(8,128)} %fusion.5) | copy-start | bytes 6291460
  211.0 5.4 %copy-start.6 = (u32[128]{0:T(128)S(1)}, u32[128]{0:T(128)}, u32[]{:S(2)}) copy-start(u32[128]{0:T(128)} %constant.22) | copy-start | bytes 1540
  211.0 100.3 %all-to-all-start.3 = ((bf16[32,16,4096]{2,1,0:T(8,128)(2,1)}), bf16[32,16,4096]{2,1,0:T(8,128)(2,1)}, u32[]{:S(2)}, u32[]{:S(2)}) async-start(bf16[32,16,4096]{2,1,0:T(8,128)(2,1)} %bitcast.86), calls=%async_computation.3 | async-start | bytes 8388608 | tf_op jit(solution)/shard_map/all_to_all | solution.py:76
  311.3 29.2 %copy-start.1 = (bf16[128,4096]{1,0:T(8,128)(2,1)S(1)}, bf16[128,4096]{1,0:T(8,128)(2,1)}, u32[]{:S(2)}) copy-start(bf16[128,4096]{1,0:T(8,128)(2,1)} %param.7) | copy-start | bytes 3145732
Sparse Core Ops, SparseCore 0:
  165.5 128.3 all-reduce.2
Sparse Core Ops, SparseCore 1:
  179.0 78.1 reduce-scatter.4
  260.0 80.5 reduce-scatter.2
where the time goes:
time: 349 us; the launch traced here: 348 us
  waiting for transfers between devices  195 us (56%)
  matrix products  73.7 us (21%)
  starting transfers between devices  34.4 us (10%)
  blocking collectives  16 us (5%)
  between operations  15.7 us (4%)
  other arithmetic  9.26 us (3%)
  local copies, waits for them, and re-layouts  3.56 us (1%)
    unnamed x4, waiting for transfers between devices  76.9 us
    all_to_all x1, waiting for transfers between devices, on_device(): lax.all_to_all(send_rows, 'expert', split_axis=0, concat_axis=0, tiled=True)  47 us
    all_to_all x1, waiting for transfers between devices, on_device(): lax.all_to_all(send_grads, 'expert', split_axis=0, concat_axis=0, tiled=T...  38.3 us
    reduce_scatter x1, waiting for transfers between devices, on_device(): lax.psum_scatter(lax.dot_general(rows_in, pre_grad, contract, preferred_e...  21.4 us
    psum x1, blocking collectives, on_device(): router_grad = lax.psum(own_column, 'dp')  16 us
    dot_general x1, matrix products, on_device(): pre = jnp.dot(rows_in, w_up, preferred_element_type=jnp.float32)  10.5 us
    dot_general x1, matrix products, on_device(): lax.dot_general(active, w_down, trailing, preferred_element_type=jnp.floa...  9.96 us
    all_to_all x1, starting transfers between devices, on_device(): lax.all_to_all(send_rows, 'expert', split_axis=0, concat_axis=0, tiled=True)  9.62 us
  transfers between devices with their start and end apart: 8, of which 6 were waited for; matrix products, arithmetic and copies ran while one was open for 20% of the time, Pallas kernels for 0%

commit v1 on v0

v1 whole, which is shorter than its diff:
```python
import jax
import jax.numpy as jnp
from jax import lax
from jax.sharding import PartitionSpec as P

TRAIL = (((1,), (1,)), ((), ()))
ROWS = (((0,), (0,)), ((), ()))


def gelu_pair(values):
    inner = 0.7978845608 * (values + 0.044715 * values * values * values)
    tangent = jnp.tanh(inner)
    result = 0.5 * values * (1.0 + tangent)
    slope = 0.5 * (1.0 + tangent) + 0.5 * values * (1.0 - tangent * tangent) * 0.7978845608 * (
        1.0 + 3.0 * 0.044715 * values * values
    )
    return (result, slope)


def on_device(tokens, out_grad, route_slots, expert_counts, router_weight, up_weight, down_weight):
    experts = lax.axis_size("expert")
    n_dp = lax.axis_size("dp")
    me = lax.axis_index("expert")
    shard = lax.axis_index("dp")
    tok_rows, width = tokens.shape
    slots = route_slots[0, 0]
    per_slot = slots.shape[1]
    received = experts * per_slot
    highest = lax.Precision.HIGHEST
    piece = width // n_dp
    swap_a = [(0, 1), (1, 0), (2, 3), (3, 2)]
    swap_b = [(0, 3), (3, 0), (1, 2), (2, 1)]

    picks = slots[:, :, None] == jnp.arange(tok_rows, dtype=jnp.int32)[None, None, :]
    pick_half = picks.astype(jnp.bfloat16).reshape(received, tok_rows)

    def dispatch(rows):
        return lax.all_to_all(
            rows.reshape(experts, per_slot, width), "expert", split_axis=0, concat_axis=0, tiled=True
        ).reshape(received, width)

    with jax.named_scope("send_tokens"):
        rows_in = dispatch(
            jnp.dot(pick_half, tokens, preferred_element_type=jnp.float32).astype(jnp.bfloat16)
        )
    with jax.named_scope("send_grads"):
        logits = jnp.dot(tokens.astype(jnp.float32), router_weight, precision=highest)
        counts = jnp.maximum(expert_counts, 1).astype(jnp.float32)
        scaled = jax.nn.sigmoid(logits) / counts[:, None]
        weight_slot = jnp.sum(jnp.where(picks, scaled.T[:, None, :], 0.0), axis=2).reshape(received)
        picked = jnp.dot(pick_half, out_grad, preferred_element_type=jnp.float32)
        dout = dispatch((weight_slot[:, None] * picked).astype(jnp.bfloat16))

    def part(rows, index):
        return lax.dynamic_slice(rows, (0, index * piece), (received, piece))

    mate_a = shard ^ 1
    mate_b = n_dp - 1 - shard
    far = n_dp - 1 - mate_a
    w_up = up_weight[0]
    w_down = down_weight[0]
    with jax.named_scope("share_tokens"):
        rows_far = lax.ppermute(
            jnp.stack([part(rows_in, mate_a), part(rows_in, far)]), "dp", swap_a
        )
    with jax.named_scope("forward"):
        pre = jnp.dot(rows_in, w_up, preferred_element_type=jnp.float32)
        active, slope = gelu_pair(pre)
        active = active.astype(jnp.bfloat16)
        active_far = lax.ppermute(active, "dp", swap_b)
        column = lax.dynamic_slice(router_weight, (0, me), (width, 1))[:, 0]
        rows_float = rows_in.astype(jnp.float32)
        gate = jax.nn.sigmoid(jnp.sum(rows_float * column[None, :], axis=1))
    with jax.named_scope("share_grads"):
        dout_far = lax.ppermute(jnp.stack([part(dout, mate_b), part(dout, far)]), "dp", swap_b)
    with jax.named_scope("backward"):
        act_grad = jnp.dot(dout, w_down, preferred_element_type=jnp.float32)
        logit_grad = (1.0 - gate) * jnp.sum(active.astype(jnp.float32) * act_grad, axis=1)
        pre_grad = (act_grad * slope).astype(jnp.bfloat16)
        pre_grad_far = lax.ppermute(pre_grad, "dp", swap_a)
        row_grad = lax.dot_general(pre_grad, w_up, TRAIL, preferred_element_type=jnp.float32)
        row_grad = (row_grad + logit_grad[:, None] * column[None, :]).astype(jnp.bfloat16)
    with jax.named_scope("return_rows"):
        back_rows = dispatch(row_grad)
    with jax.named_scope("weight_grads"):

        def product(left, right, left_far, right_far):
            return lax.dot_general(
                left, right, ROWS, preferred_element_type=jnp.float32
            ) + lax.dot_general(left_far, right_far, ROWS, preferred_element_type=jnp.float32)

        down_send = product(part(dout, mate_a), active, dout_far[1], active_far)
        down_got = lax.ppermute(down_send.astype(jnp.bfloat16), "dp", swap_a)
        up_send = product(part(rows_in, mate_b), pre_grad, rows_far[1], pre_grad_far)
        up_got = lax.ppermute(up_send.astype(jnp.bfloat16), "dp", swap_b)
        down_own = product(part(dout, shard), active, dout_far[0], active_far)
        up_own = product(part(rows_in, shard), pre_grad, rows_far[0], pre_grad_far)
        down_sum = (down_own + down_got.astype(jnp.float32)).astype(jnp.bfloat16)
        up_sum = (up_own + up_got.astype(jnp.float32)).astype(jnp.bfloat16)
    with jax.named_scope("router_grad"):
        terms = jnp.sum(rows_float * logit_grad[:, None], axis=0)
        terms = terms + lax.ppermute(terms, "dp", swap_a)
        terms = terms + lax.ppermute(terms, "dp", swap_b)
    with jax.named_scope("tokens_grad"):
        tokens_grad = lax.dot_general(
            pick_half, back_rows, ROWS, preferred_element_type=jnp.float32
        ).astype(jnp.bfloat16)
    return (tokens_grad, up_sum[None], down_sum[None], terms[:, None])


def solution(mesh):
    return jax.shard_map(
        on_device,
        mesh=mesh,
        in_specs=(
            P(("dp", "expert"), None),
            P(("dp", "expert"), None),
            P("dp", "expert", None, None),
            P(("dp", "expert")),
            P(),
            P("expert", None, None),
            P("expert", None, None),
        ),
        out_specs=(
            P(("dp", "expert"), None),
            P("expert", "dp", None),
            P("expert", "dp", None),
            P(None, "expert"),
        ),
        check_vma=False,
    )
```

time: 349 us -> 320 us (0.917)
  blocking collectives: 16 us -> 0 us
  waiting for transfers between devices: 195 us -> 179 us
  between operations: 15.7 us -> 0.81 us
  other arithmetic: 9.26 us -> 21.6 us
    ppermute x0 -> x8, waiting for transfers between devices: none -> 88.6 us  [the longest x1 39.9 us: on_device(): pre_grad_far = lax.ppermute(pre_grad, 'dp', swap_a)]
    unnamed x4 -> x0, waiting for transfers between devices: 76.9 us -> none
    reduce_scatter x2 -> x0, waiting for transfers between devices: 21.4 us -> none  [the longest x1 21.4 us: on_device(): lax.psum_scatter(lax.dot_general(rows_in, pre_grad, contract, preferred_e...]
    psum x1 -> x0, blocking collectives: 16 us -> none  [on_device(): router_grad = lax.psum(own_column, 'dp')]
    ppermute x0 -> x8, starting transfers between devices: none -> 10.1 us  [the longest x1 2.73 us: on_device(): lax.ppermute(jnp.stack([part(dout, mate_b), part(dout, far)]), 'dp', swap_b)]
    broadcast_in_dim x0 -> x2, other arithmetic: none -> 9.78 us  [on_device(): return (tokens_grad, up_sum[None], down_sum[None], terms[:, None])]
    all_to_all x5 -> x3, starting transfers between devices: 34.2 us -> 25.4 us  [dispatch(): lax.all_to_all(rows.reshape(experts, per_slot, width), 'expert', split_ax...]
    convert_element_type x6 -> x1, other arithmetic: 9.11 us -> 0.75 us  [on_device(): counts = jnp.maximum(expert_counts, 1).astype(jnp.float32)]
  transfers between devices with their start and end apart: 8 -> 11, of which waited for: 6 -> 5; matrix products, arithmetic and copies ran while one was open for 20% -> 28% of each run, Pallas kernels for 0% -> 0%
where the time goes in v1:
time: 320 us; the launch traced here: 317 us
  waiting for transfers between devices  179 us (56%)
  matrix products  74.7 us (23%)
  starting transfers between devices  35.5 us (11%)
  other arithmetic  21.6 us (7%)
  local copies, waits for them, and re-layouts  5.57 us (2%)
    all_to_all x3, waiting for transfers between devices, dispatch(): lax.all_to_all(rows.reshape(experts, per_slot, width), 'expert', split_ax...  90.5 us
    ppermute x1, waiting for transfers between devices, on_device(): pre_grad_far = lax.ppermute(pre_grad, 'dp', swap_a)  39.9 us
    ppermute x1, waiting for transfers between devices, on_device(): terms = terms + lax.ppermute(terms, 'dp', swap_b)  35 us
    all_to_all x3, starting transfers between devices, dispatch(): lax.all_to_all(rows.reshape(experts, per_slot, width), 'expert', split_ax...  25.4 us
    dot_general x4, matrix products, product(): lax.dot_general(left, right, ROWS, preferred_element_type=jnp.float32)  14.4 us
    dot_general x4, matrix products, product(): lax.dot_general(left_far, right_far, ROWS, preferred_element_type=jnp.flo...  14.4 us
    ppermute x1, waiting for transfers between devices, on_device(): active_far = lax.ppermute(active, 'dp', swap_b)  13.7 us
    dot_general x1, matrix products, on_device(): act_grad = jnp.dot(dout, w_down, preferred_element_type=jnp.float32)  11.7 us
  transfers between devices with their start and end apart: 11, of which 5 were waited for; matrix products, arithmetic and copies ran while one was open for 28% of the time, Pallas kernels for 0%

profile of v1, /device:TPU:1, one launch (start us, length us, event | category | flops | bytes accessed | tf_op | source)
XLA Modules:
  0.0 317.2 jit_solution(4032441151495429898)
XLA Ops:
  0.6 0.0 copy-start
  0.6 0.7 maximum_convert_fusion
  1.4 0.8 copy.15
  2.2 0.0 copy-done
  2.2 2.1 fusion.24
  4.3 1.0 select_reduce_fusion
  5.3 0.1 copy.14
  5.3 0.1 mul.121
  5.4 0.1 eq.28
  5.5 4.5 %multiply_convert_fusion = bf16[512,4096]{1,0:T(8,128)(2,1)} fusion(bf16[128,4096]{1,0:T(8,128)(2,1)} %param.8, f32[512]{0:T(512)S(1)} %mul.121, s32[512]{0:T(512)S(1)} %eq.28), kind=kOutput, calls=%fused_computation.11 | convolution fusion | flops 541130752 | bytes 5246976 | tf_op jit(solution)/shard_map/send_grads/dot_general | solution.py:51
  10.0 9.5 %all-to-all-start = ((bf16[32,16,4096]{2,1,0:T(8,128)(2,1)}), bf16[32,16,4096]{2,1,0:T(8,128)(2,1)}, u32[]{:S(2)}, u32[]{:S(2)}) async-start(bf16[32,16,4096]{2,1,0:T(8,128)(2,1)} %bitcast.66), calls=%async_computation | async-start | bytes 8388608 | tf_op jit(solution)/shard_map/send_grads/all_to_all | solution.py:38
  19.5 3.3 %convolution_convert_fusion = bf16[512,4096]{1,0:T(8,128)(2,1)} fusion(bf16[128,4096]{1,0:T(8,128)(2,1)S(1)} %copy-done, s32[512]{0:T(512)S(1)} %eq.28), kind=kOutput, calls=%fused_computation.12 | convolution fusion | flops 539033600 | bytes 5244928 | tf_op jit(solution)/shard_map/send_tokens/dot_general | solution.py:44
  22.8 47.0 %all-to-all-done = bf16[32,16,4096]{2,1,0:T(8,128)(2,1)} async-done(((bf16[32,16,4096]{2,1,0:T(8,128)(2,1)}), bf16[32,16,4096]{2,1,0:T(8,128)(2,1)}, u32[]{:S(2)}, u32[]{:S(2)}) %all-to-all-start) | async-done | bytes 4194336 | tf_op jit(solution)/shard_map/send_grads/all_to_all | solution.py:38
  69.8 8.0 %all-to-all-start.1 = ((bf16[32,16,4096]{2,1,0:T(8,128)(2,1)}), bf16[32,16,4096]{2,1,0:T(8,128)(2,1)}, u32[]{:S(2)}, u32[]{:S(2)}) async-start(bf16[32,16,4096]{2,1,0:T(8,128)(2,1)} %bitcast.65), calls=%async_computation.1 | async-start | bytes 8388608 | tf_op jit(solution)/shard_map/send_tokens/all_to_all | solution.py:38
  77.7 0.9 constant_dynamic-slice_fusion
  78.7 1.7 dynamic-slice_bitcast_fusion.1
  80.4 1.5 pad_maximum_fusion.1
  81.9 2.7 collective-permute-start.3
  84.6 43.5 %all-to-all-done.1 = bf16[32,16,4096]{2,1,0:T(8,128)(2,1)} async-done(((bf16[32,16,4096]{2,1,0:T(8,128)(2,1)}), bf16[32,16,4096]{2,1,0:T(8,128)(2,1)}, u32[]{:S(2)}, u32[]{:S(2)}) %all-to-all-start.1) | async-done | bytes 4194336 | tf_op jit(solution)/shard_map/send_tokens/all_to_all | solution.py:38
  128.1 8.1 %fusion.4 = f32[512,1024]{1,0:T(8,128)S(1)} fusion(bf16[512,4096]{1,0:T(8,128)(2,1)} %bitcast.5, bf16[1,4096,1024]{2,1,0:T(8,128)(2,1)} %param.12), kind=kOutput, calls=%fused_computation.6 | convolution fusion | flops 4294967296 | bytes 14680064 | tf_op jit(solution)/shard_map/forward/dot_general | solution.py:67
  136.3 11.7 %multiply_reduce_fusion = (f32[512]{0:T(512)S(1)}, bf16[512,1024]{1,0:T(8,128)(2,1)}, bf16[512,1024]{1,0:T(8,128)(2,1)}) fusion(f32[512,1024]{1,0:T(8,128)S(1)} %fusion.4, bf16[512,4096]{1,0:T(8,128)(2,1)} %bitcast.2, bf16[1,4096,1024]{2,1,0:T(8,128)(2,1)} %param.13), kind=kOutput, calls=%fused_computation.33 | convolution fusion | flops 4307549696 | bytes 16779264 | tf_op jit(solution)/shard_map/backward/dot_general | solution.py:77
  148.0 0.1 reduce_sum.41
  148.1 3.1 fusion
  151.2 0.1 reshape.70
  151.3 10.2 %add_convert_fusion = bf16[512,4096]{1,0:T(8,128)(2,1)} fusion(bf16[512,1024]{1,0:T(8,128)(2,1)} %get-tuple-element.10, bf16[1,4096,1024]{2,1,0:T(8,128)(2,1)} %param.12, f32[4096]{0:T(1024)S(1)} %bitcast.69, f32[512]{0:T(512)S(1)} %mul.144), kind=kOutput, calls=%fused_computation.10 | convolution fusion | flops 4301258752 | bytes 13649920 | tf_op jit(solution)/shard_map/backward/dot_general | solution.py:81
  161.5 8.0 %all-to-all-start.2 = ((bf16[32,16,4096]{2,1,0:T(8,128)(2,1)}), bf16[32,16,4096]{2,1,0:T(8,128)(2,1)}, u32[]{:S(2)}, u32[]{:S(2)}) async-start(bf16[32,16,4096]{2,1,0:T(8,128)(2,1)} %bitcast.67), calls=%async_computation.2 | async-start | bytes 8388608 | tf_op jit(solution)/shard_map/return_rows/all_to_all | solution.py:38
  169.5 1.7 dynamic-slice_bitcast_fusion.3
  171.2 1.5 pad_maximum_fusion
  172.7 1.3 collective-permute-start
  174.0 0.2 collective-permute-start.1
  174.2 2.7 collective-permute-start.4
  176.9 3.4 %fusion.1 = f32[4096]{0:T(1024)S(1)} fusion(bf16[32,16,4096]{2,1,0:T(8,128)(2,1)} %all-to-all-done.1, f32[32,16]{1,0:T(8,128)S(1)} %get-tuple-element.11), kind=kLoop, calls=%fused_computation.3 | loop fusion | flops 6287360 | bytes 4212736 | tf_op jit(solution)/shard_map/router_grad/reduce_sum | solution.py:101
  180.3 0.0 copy-start.6
  180.3 0.1 collective-permute-start.6
  180.4 2.9 fusion.27
  183.3 0.0 copy-done.6
  183.3 2.5 fusion.31
  185.8 13.7 %collective-permute-done.4 = bf16[512,1024]{1,0:T(8,128)(2,1)S(1)} collective-permute-done((bf16[512,1024]{1,0:T(8,128)(2,1)}, bf16[512,1024]{1,0:T(8,128)(2,1)S(1)}, u32[]{:S(2)}, u32[]{:S(2)}) %collective-permute-start.4) | collective-permute-done | bytes 1048608 | tf_op jit(solution)/shard_map/forward/ppermute | solution.py:70
  199.5 0.0 collective-permute-done.3
  199.5 2.7 add_convert_fusion.2
  202.2 0.0 collective-permute-start.5
  202.2 39.9 %collective-permute-done.1 = bf16[512,1024]{1,0:T(8,128)(2,1)S(1)} collective-permute-done((bf16[512,1024]{1,0:T(8,128)(2,1)}, bf16[512,1024]{1,0:T(8,128)(2,1)S(1)}, u32[]{:S(2)}, u32[]{:S(2)}) %collective-permute-start.1) | collective-permute-done | bytes 1048608 | tf_op jit(solution)/shard_map/backward/ppermute | solution.py:80
  242.2 0.0 collective-permute-done
  242.2 3.9 %add_convert_fusion.4 = bf16[1024,1024]{1,0:T(8,128)(2,1)} fusion(f32[1024,1024]{1,0:T(8,128)S(1)} %fusion.31, bf16[512,1024]{1,0:T(8,128)(2,1)S(1)} %collective-permute-done.1, bf16[2,512,1024]{2,1,0:T(8,128)(2,1)} %collective-permute-done), kind=kOutput, calls=%fused_computation.19 | convolution fusion | flops 1075838976 | bytes 8388608 | tf_op jit(solution)/shard_map/weight_grads/dot_general | solution.py:90
  246.1 2.7 collective-permute-start.2
  248.8 0.0 copy-done.7
  248.8 4.5 %fusion.29 = f32[1024,1024]{1,0:T(8,128)} fusion(bf16[512,1024]{1,0:T(8,128)(2,1)S(1)} %copy-done.7, bf16[512,4096]{1,0:T(8,128)(2,1)} %bitcast.2, s32[]{:T(128)S(6)} %select_n.25), kind=kOutput, calls=%fused_computation.50 | convolution fusion | flops 1073741824 | bytes 6291460 | tf_op jit(solution)/shard_map/weight_grads/dot_general | solution.py:88
  253.3 0.0 collective-permute-done.6
  253.3 0.3 collective-permute-start.7
  253.6 4.5 %fusion.33 = f32[1024,1024]{1,0:T(8,128)} fusion(bf16[512,1024]{1,0:T(8,128)(2,1)S(1)} %copy-done.6, bf16[512,4096]{1,0:T(8,128)(2,1)} %bitcast.5, s32[]{:T(128)S(6)} %select_n.25), kind=kOutput, calls=%fused_computation.56 | convolution fusion | flops 1073741824 | bytes 6291460 | tf_op jit(solution)/shard_map/weight_grads/dot_general | solution.py:88
  258.1 35.0 %collective-permute-done.7 = f32[4096]{0:T(1024)S(1)} collective-permute-done((f32[4096]{0:T(1024)S(1)}, f32[4096]{0:T(1024)S(1)}, u32[]{:S(2)}, u32[]{:S(2)}) %collective-permute-start.7) | collective-permute-done | bytes 16416 | tf_op jit(solution)/shard_map/router_grad/ppermute | solution.py:103
  293.1 0.6 add.91
  293.7 3.3 %fusion.25 = f32[1024,1024]{1,0:T(8,128)} fusion(bf16[512,1024]{1,0:T(8,128)(2,1)S(1)} %collective-permute-done.4, bf16[2,512,1024]{2,1,0:T(8,128)(2,1)S(1)} %collective-permute-done.3), kind=kOutput, calls=%fused_computation.42 | convolution fusion | flops 1073741824 | bytes 6291456 | tf_op jit(solution)/shard_map/weight_grads/dot_general | solution.py:90
  296.9 4.5 %fusion.26 = f32[1024,1024]{1,0:T(8,128)} fusion(bf16[512,1024]{1,0:T(8,128)(2,1)S(1)} %collective-permute-done.1, bf16[2,512,1024]{2,1,0:T(8,128)(2,1)} %collective-permute-done), kind=kOutput, calls=%fused_computation.45 | convolution fusion | flops 1073741824 | bytes 6291456 | tf_op jit(solution)/shard_map/weight_grads/dot_general | solution.py:90
  301.4 0.0 all-to-all-done.2
  301.4 0.0 copy-done.5
  301.4 6.0 %fusion.10 = bf16[128,4096]{1,0:T(8,128)(2,1)} fusion(bf16[32,16,4096]{2,1,0:T(8,128)(2,1)} %all-to-all-done.2, s32[32,16]{0,1:T(8,128)S(1)} %bitcast.71), kind=kOutput, calls=%fused_computation.14 | convolution fusion | flops 537460736 | bytes 5244928 | tf_op jit(solution)/shard_map/tokens_grad/dot_general | solution.py:105
  307.4 0.0 collective-permute-done.5
  307.4 0.0 copy-start.1
  307.4 5.6 %fusion.20 = bf16[1,1024,1024]{2,1,0:T(8,128)(2,1)} fusion(bf16[1024,1024]{1,0:T(8,128)(2,1)} %collective-permute-done.5, f32[1024,1024]{1,0:T(8,128)} %fusion.29, f32[1024,1024]{1,0:T(8,128)S(1)} %copy-done.3), kind=kLoop, calls=%fused_computation.30 | loop fusion | flops 4194304 | bytes 12582912 | tf_op jit(solution)/shard_map/broadcast_in_dim | solution.py:108
  313.0 0.0 collective-permute-done.2
  313.0 0.0 copy-done.2
  313.0 4.2 %fusion.19 = bf16[1,1024,1024]{2,1,0:T(8,128)(2,1)} fusion(bf16[1024,1024]{1,0:T(8,128)(2,1)} %collective-permute-done.2, f32[1024,1024]{1,0:T(8,128)S(1)} %copy-done.4, f32[1024,1024]{1,0:T(8,128)S(1)} %copy-done.2), kind=kLoop, calls=%fused_computation.29 | loop fusion | flops 4194304 | bytes 12582912 | tf_op jit(solution)/shard_map/broadcast_in_dim | solution.py:108
  317.2 0.0 copy-done.1
  (10 shorter events, 0.1 us)
Async XLA Ops:
  0.6 1.5 copy-start
  10.0 59.8 %all-to-all-start = ((bf16[32,16,4096]{2,1,0:T(8,128)(2,1)}), bf16[32,16,4096]{2,1,0:T(8,128)(2,1)}, u32[]{:S(2)}, u32[]{:S(2)}) async-start(bf16[32,16,4096]{2,1,0:T(8,128)(2,1)} %bitcast.66), calls=%async_computation | async-start | bytes 8388608 | tf_op jit(solution)/shard_map/send_grads/all_to_all | solution.py:38
  69.8 58.4 %all-to-all-start.1 = ((bf16[32,16,4096]{2,1,0:T(8,128)(2,1)}), bf16[32,16,4096]{2,1,0:T(8,128)(2,1)}, u32[]{:S(2)}, u32[]{:S(2)}) async-start(bf16[32,16,4096]{2,1,0:T(8,128)(2,1)} %bitcast.65), calls=%async_computation.1 | async-start | bytes 8388608 | tf_op jit(solution)/shard_map/send_tokens/all_to_all | solution.py:38
  81.9 117.6 %collective-permute-start.3 = (bf16[2,512,1024]{2,1,0:T(8,128)(2,1)}, bf16[2,512,1024]{2,1,0:T(8,128)(2,1)S(1)}, u32[]{:S(2)}, u32[]{:S(2)}) collective-permute-start(bf16[2,512,1024]{2,1,0:T(8,128)(2,1)} %pad_maximum_fusion.1), channel_id=1, source_target_pairs={{0,96},{96,0},{32,64},{64,32},{1,97},{97,1},{33,65},{65,33},{2,98}... | collective-permute-start | bytes 6291464 | tf_op jit(solution)/shard_map/share_grads/ppermute | solution.py:75
  161.5 139.9 %all-to-all-start.2 = ((bf16[32,16,4096]{2,1,0:T(8,128)(2,1)}), bf16[32,16,4096]{2,1,0:T(8,128)(2,1)}, u32[]{:S(2)}, u32[]{:S(2)}) async-start(bf16[32,16,4096]{2,1,0:T(8,128)(2,1)} %bitcast.67), calls=%async_computation.2 | async-start | bytes 8388608 | tf_op jit(solution)/shard_map/return_rows/all_to_all | solution.py:38
  172.7 69.5 %collective-permute-start = (bf16[2,512,1024]{2,1,0:T(8,128)(2,1)}, bf16[2,512,1024]{2,1,0:T(8,128)(2,1)}, u32[]{:S(2)}, u32[]{:S(2)}) collective-permute-start(bf16[2,512,1024]{2,1,0:T(8,128)(2,1)} %pad_maximum_fusion), channel_id=1, source_target_pairs={{0,32},{32,0},{64,96},{96,64},{1,33},{33,1},{65,97},{97,65},{2,34}... | collective-permute-start | bytes 6291464 | tf_op jit(solution)/shard_map/share_tokens/ppermute | solution.py:63
  174.0 68.2 %collective-permute-start.1 = (bf16[512,1024]{1,0:T(8,128)(2,1)}, bf16[512,1024]{1,0:T(8,128)(2,1)S(1)}, u32[]{:S(2)}, u32[]{:S(2)}) collective-permute-start(bf16[512,1024]{1,0:T(8,128)(2,1)} %get-tuple-element.10), channel_id=1, source_target_pairs={{0,32},{32,0},{64,96},{96,64},{1,33},{33,1},{65,97},{97,65},{2,34}... | collective-permute-start | bytes 3145736 | tf_op jit(solution)/shard_map/backward/ppermute | solution.py:80
  174.2 25.3 %collective-permute-start.4 = (bf16[512,1024]{1,0:T(8,128)(2,1)}, bf16[512,1024]{1,0:T(8,128)(2,1)S(1)}, u32[]{:S(2)}, u32[]{:S(2)}) collective-permute-start(bf16[512,1024]{1,0:T(8,128)(2,1)} %get-tuple-element.5), channel_id=1, source_target_pairs={{0,96},{96,0},{32,64},{64,32},{1,97},{97,1},{33,65},{65,33},{2,98}... | collective-permute-start | bytes 3145736 | tf_op jit(solution)/shard_map/forward/ppermute | solution.py:70
  180.3 3.0 copy-start.6
  180.3 73.0 %collective-permute-start.6 = (f32[4096]{0:T(1024)S(1)}, f32[4096]{0:T(1024)S(1)}, u32[]{:S(2)}, u32[]{:S(2)}) collective-permute-start(f32[4096]{0:T(1024)S(1)} %fusion.1), channel_id=1, source_target_pairs={{0,32},{32,0},{64,96},{96,64},{1,33},{33,1},{65,97},{97,65},{2,34}... | collective-permute-start | bytes 49160 | tf_op jit(solution)/shard_map/router_grad/ppermute | solution.py:102
  202.2 46.6 %copy-start.7 = (bf16[512,1024]{1,0:T(8,128)(2,1)S(1)}, bf16[512,1024]{1,0:T(8,128)(2,1)}, u32[]{:S(2)}) copy-start(bf16[512,1024]{1,0:T(8,128)(2,1)} %get-tuple-element.5) | copy-start | bytes 3145732
  202.2 105.2 %collective-permute-start.5 = (bf16[1024,1024]{1,0:T(8,128)(2,1)}, bf16[1024,1024]{1,0:T(8,128)(2,1)}, u32[]{:S(2)}, u32[]{:S(2)}) collective-permute-start(bf16[1024,1024]{1,0:T(8,128)(2,1)} %add_convert_fusion.2), channel_id=1, source_target_pairs={{0,32},{32,0},{64,96},{96,64},{1,33},{33,1},{65,97},{97,65},{2,34}... | collective-permute-start | bytes 6291464 | tf_op jit(solution)/shard_map/weight_grads/ppermute | solution.py:93
  246.1 66.9 %collective-permute-start.2 = (bf16[1024,1024]{1,0:T(8,128)(2,1)}, bf16[1024,1024]{1,0:T(8,128)(2,1)}, u32[]{:S(2)}, u32[]{:S(2)}) collective-permute-start(bf16[1024,1024]{1,0:T(8,128)(2,1)} %add_convert_fusion.4), channel_id=1, source_target_pairs={{0,96},{96,0},{32,64},{64,32},{1,97},{97,1},{33,65},{65,33},{2,98}... | collective-permute-start | bytes 6291464 | tf_op jit(solution)/shard_map/weight_grads/ppermute | solution.py:95
  253.3 39.8 %collective-permute-start.7 = (f32[4096]{0:T(1024)S(1)}, f32[4096]{0:T(1024)S(1)}, u32[]{:S(2)}, u32[]{:S(2)}) collective-permute-start(f32[4096]{0:T(1024)S(1)} %add.90), channel_id=1, source_target_pairs={{0,96},{96,0},{32,64},{64,32},{1,97},{97,1},{33,65},{65,33},{2,98}... | collective-permute-start | bytes 49160 | tf_op jit(solution)/shard_map/router_grad/ppermute | solution.py:103
  296.9 4.5 %copy-start.5 = (s32[1,1,32,16]{2,3,1,0:T(8,128)S(1)}, s32[1,1,32,16]{2,3,1,0:T(8,128)}, u32[]{:S(2)}) copy-start(s32[1,1,32,16]{2,3,1,0:T(8,128)} %param.9) | copy-start | bytes 6148
  301.4 6.0 %copy-start.3 = (f32[1024,1024]{1,0:T(8,128)S(1)}, f32[1024,1024]{1,0:T(8,128)}, u32[]{:S(2)}) copy-start(f32[1024,1024]{1,0:T(8,128)} %fusion.25) | copy-start | bytes 12582916
  307.4 5.6 %copy-start.2 = (f32[1024,1024]{1,0:T(8,128)S(1)}, f32[1024,1024]{1,0:T(8,128)}, u32[]{:S(2)}) copy-start(f32[1024,1024]{1,0:T(8,128)} %fusion.26) | copy-start | bytes 12582916
  307.4 5.6 %copy-start.4 = (f32[1024,1024]{1,0:T(8,128)S(1)}, f32[1024,1024]{1,0:T(8,128)}, u32[]{:S(2)}) copy-start(f32[1024,1024]{1,0:T(8,128)} %fusion.33) | copy-start | bytes 12582916
  307.4 9.8 %copy-start.1 = (bf16[128,4096]{1,0:T(8,128)(2,1)S(1)}, bf16[128,4096]{1,0:T(8,128)(2,1)}, u32[]{:S(2)}) copy-start(bf16[128,4096]{1,0:T(8,128)(2,1)} %param.7) | copy-start | bytes 3145732

commit v2 on v1

v2 whole, which is shorter than its diff:
```python
import functools

import jax
import jax.numpy as jnp
from jax import lax
from jax.experimental import pallas as pl
from jax.experimental.pallas import tpu as pltpu
from jax.sharding import PartitionSpec as P

MESH = pl.DeviceIdType.MESH
TRAIL = (((1,), (1,)), ((), ()))
ROWS = (((0,), (0,)), ((), ()))
WAVES = (
    ((1, 1), (3, 3), (1, 3), (3, 1)),
    ((0, 0), (2, 2), (2, 0), (0, 2)),
    ((1, 0), (3, 0), (1, 2), (3, 2)),
    ((0, 1), (0, 3), (2, 1), (2, 3)),
)
STEPS = tuple((dz, dx, dc) for wave in WAVES for dz, dx in wave for dc in (0, 1))
SELF = STEPS.index((0, 0, 0))
PER_WAVE = 8
PIECES = 4


def shifted(me, step, sign):
    dz, dx, dc = step
    z, x, c = me // 8, (me // 2) % 4, me % 2
    z = (z + sign * dz + 4) % 4
    x = (x + sign * dx + 4) % 4
    c = (c + sign * dc + 2) % 2
    return (z * 4 + x) * 2 + c


def gelu_pair(values):
    inner = 0.7978845608 * (values + 0.044715 * values * values * values)
    tangent = jnp.tanh(inner)
    result = 0.5 * values * (1.0 + tangent)
    slope = 0.5 * (1.0 + tangent) + 0.5 * values * (1.0 - tangent * tangent) * 0.7978845608 * (
        1.0 + 3.0 * 0.044715 * values * values
    )
    return (result, slope)


def kernel(
    tokens, grads, pick, pick_back, weight, column, up_hbm, down_hbm,
    tokens_grad, up_out, down_out, terms_out,
    x_send, g_send, x_in, g_in, r_in, w_up, w_down, act, slope, dpre, logit,
    x_far, dpre_far, g_far, act_far, up_send, down_send, up_got, down_got, up_own, down_own,
    terms_a, terms_b,
    w_sem, xs_sem, xr_sem, gs_sem, gr_sem, rs_sem, rr_sem,
    xfs_sem, xfr_sem, dfs_sem, dfr_sem, gfs_sem, gfr_sem, afs_sem, afr_sem,
    ups_sem, upr_sem, dns_sem, dnr_sem, ts_sem, tr_sem, out_sem,
):
    shard = lax.axis_index("dp")
    me = lax.axis_index("expert")
    mate_a = shard + 1 - 2 * (shard % 2)
    mate_b = 3 - shard
    far = 3 - mate_a
    width = tokens.shape[1]
    hidden = act.shape[1]
    piece = width // 4
    block = 16
    wave_rows = PER_WAVE * block
    step_rows = piece // PIECES

    load_up = pltpu.make_async_copy(up_hbm, w_up, w_sem.at[0])
    load_down = pltpu.make_async_copy(down_hbm, w_down, w_sem.at[1])
    load_up.start()
    load_down.start()

    barrier = pltpu.get_barrier_semaphore()
    for step in STEPS:
        if step != (0, 0, 0):
            pl.semaphore_signal(
                barrier, inc=1, device_id=(shard, shifted(me, step, 1)), device_id_type=MESH
            )
    pl.semaphore_signal(barrier, inc=1, device_id=(mate_a, me), device_id_type=MESH)
    pl.semaphore_signal(barrier, inc=1, device_id=(mate_b, me), device_id_type=MESH)
    pl.semaphore_wait(barrier, len(STEPS) + 1)

    def span(w):
        return pl.ds(w * wave_rows, wave_rows)

    def columns(index, size=piece, offset=0):
        return pl.ds(pl.multiple_of(index * piece + offset, 128), size)

    def arrived(ref, sem):
        pltpu.make_async_copy(ref, ref, sem).wait()

    def remote(src, dst, send, recv, device):
        copy = pltpu.make_async_remote_copy(
            src_ref=src, dst_ref=dst, send_sem=send, recv_sem=recv,
            device_id=device, device_id_type=MESH,
        )
        copy.start()

    def wave_part(w):
        if SELF // PER_WAVE == w:
            return pl.ds(w * wave_rows + block, wave_rows - block)
        return span(w)

    def send_blocks(w, sign, src, dst, send, recv):
        for k in range(w * PER_WAVE, (w + 1) * PER_WAVE):
            if k != SELF:
                rows = pl.ds(k * block, block)
                remote(
                    src.at[rows], dst.at[rows], send.at[w], recv.at[w],
                    (shard, shifted(me, STEPS[k], sign)),
                )

    def own_block(w, src, dst):
        if SELF // PER_WAVE == w:
            rows = pl.ds(SELF * block, block)
            dst[rows, :] = src[rows, :]

    for w in range(4):
        @pl.loop(0, 4)
        def _(n):
            cols = columns(n)
            picked = jnp.dot(
                pick[span(w), :], tokens[:, cols], preferred_element_type=jnp.float32
            )
            x_send[span(w), cols] = picked.astype(jnp.bfloat16)

        send_blocks(w, 1, x_send, x_in, xs_sem, xr_sem)
        own_block(w, x_send, x_in)

        @pl.loop(0, 4)
        def _(n):
            cols = columns(n)
            picked = jnp.dot(
                pick[span(w), :], grads[:, cols], preferred_element_type=jnp.float32
            )
            g_send[span(w), cols] = (weight[span(w), :] * picked).astype(jnp.bfloat16)

        send_blocks(w, 1, g_send, g_in, gs_sem, gr_sem)
        own_block(w, g_send, g_in)

    load_up.wait()
    load_down.wait()
    for w in range(4):
        rows = span(w)
        arrived(x_in.at[wave_part(w)], xr_sem.at[w])
        for slot, index in ((1, far), (0, mate_a)):
            remote(
                x_in.at[rows, columns(index)], x_far.at[slot, rows],
                xfs_sem.at[w], xfr_sem.at[w], (mate_a, me),
            )

        @pl.loop(0, 4)
        def _(n):
            cols = pl.ds(pl.multiple_of(n * 256, 256), 256)
            pre = jnp.dot(x_in[rows, :], w_up[:, cols], preferred_element_type=jnp.float32)
            active, bend = gelu_pair(pre)
            act[rows, cols] = active.astype(jnp.bfloat16)
            slope[:, cols] = bend

        remote(act.at[rows], act_far.at[rows], afs_sem.at[w], afr_sem.at[w], (mate_b, me))
        gate = jnp.zeros((wave_rows, 1), jnp.float32)
        for n in range(4):
            cols = pl.ds(n * piece, piece)
            gate = gate + jnp.sum(
                x_in[rows, cols].astype(jnp.float32) * column[:, cols], axis=1, keepdims=True
            )
        closed = 1.0 - jax.nn.sigmoid(gate)
        arrived(g_in.at[wave_part(w)], gr_sem.at[w])
        for slot, index in ((1, far), (0, mate_b)):
            remote(
                g_in.at[rows, columns(index)], g_far.at[slot, rows],
                gfs_sem.at[w], gfr_sem.at[w], (mate_b, me),
            )
        logit[rows, :] = jnp.zeros((wave_rows, 1), jnp.float32)

        @pl.loop(0, 4)
        def _(n):
            cols = pl.ds(pl.multiple_of(n * 256, 256), 256)
            back = jnp.dot(g_in[rows, :], w_down[:, cols], preferred_element_type=jnp.float32)
            logit[rows, :] += jnp.sum(
                act[rows, cols].astype(jnp.float32) * back, axis=1, keepdims=True
            )
            dpre[rows, cols] = (back * slope[:, cols]).astype(jnp.bfloat16)

        remote(dpre.at[rows], dpre_far.at[rows], dfs_sem.at[w], dfr_sem.at[w], (mate_a, me))
        logit[rows, :] = logit[rows, :] * closed
        arrived(x_send.at[wave_part(w)], xs_sem.at[w])

        @pl.loop(0, 8)
        def _(n):
            cols = pl.ds(pl.multiple_of(n * 512, 512), 512)
            partial = lax.dot_general(
                dpre[rows, :], w_up[cols, :], TRAIL, preferred_element_type=jnp.float32
            )
            partial = partial + logit[rows, :] * column[:, cols]
            x_send[rows, cols] = partial.astype(jnp.bfloat16)

        send_blocks(w, -1, x_send, r_in, rs_sem, rr_sem)
        own_block(w, x_send, r_in)

    def product(left, index, right, left_far, slot, right_far, i, n):
        cols = pl.ds(pl.multiple_of(n * 512, 512), 512)
        offset = i * step_rows
        near = lax.dot_general(
            left[:, columns(index, step_rows, offset)], right[:, cols], ROWS,
            preferred_element_type=jnp.float32,
        )
        other = lax.dot_general(
            left_far[slot, :, pl.ds(offset, step_rows)], right_far[:, cols], ROWS,
            preferred_element_type=jnp.float32,
        )
        return cols, near + other

    for w in range(4):
        arrived(g_far.at[:, span(w)], gfr_sem.at[w])
        arrived(act_far.at[span(w)], afr_sem.at[w])
        arrived(x_far.at[:, span(w)], xfr_sem.at[w])
        arrived(dpre_far.at[span(w)], dfr_sem.at[w])
    for i in range(PIECES):
        part = pl.ds(i * step_rows, step_rows)

        @pl.loop(0, 2)
        def _(n):
            cols, value = product(g_in, mate_a, act, g_far, 1, act_far, i, n)
            down_send[part, cols] = value.astype(jnp.bfloat16)

        remote(down_send.at[part], down_got.at[part], dns_sem.at[i], dnr_sem.at[i], (mate_a, me))

        @pl.loop(0, 2)
        def _(n):
            cols, value = product(x_in, mate_b, dpre, x_far, 1, dpre_far, i, n)
            up_send[part, cols] = value.astype(jnp.bfloat16)

        remote(up_send.at[part], up_got.at[part], ups_sem.at[i], upr_sem.at[i], (mate_b, me))

    for n in range(8):
        cols = pl.ds(n * 512, 512)
        terms_a[0:1, cols] = jnp.sum(
            x_in[:, cols].astype(jnp.float32) * logit[...], axis=0, keepdims=True
        )
    remote(terms_a.at[0:1], terms_a.at[1:2], ts_sem.at[0], tr_sem.at[0], (mate_a, me))
    arrived(terms_a.at[1:2], tr_sem.at[0])
    terms_b[0:1, :] = terms_a[0:1, :] + terms_a[1:2, :]
    remote(terms_b.at[0:1], terms_b.at[1:2], ts_sem.at[1], tr_sem.at[1], (mate_b, me))
    arrived(terms_b.at[1:2], tr_sem.at[1])
    terms_out[...] = terms_b[0:1, :] + terms_b[1:2, :]

    for i in range(PIECES):
        part = pl.ds(i * step_rows, step_rows)
        if i == PIECES - 1:
            for w in range(4):
                arrived(r_in.at[wave_part(w)], rr_sem.at[w])

            @pl.loop(0, 8)
            def _(n):
                cols = pl.ds(pl.multiple_of(n * 512, 512), 512)
                tokens_grad[:, cols] = jnp.dot(
                    pick_back[...], r_in[:, cols], preferred_element_type=jnp.float32
                ).astype(jnp.bfloat16)

        arrived(down_got.at[part], dnr_sem.at[i])

        @pl.loop(0, 2)
        def _(n):
            cols, value = product(g_in, shard, act, g_far, 0, act_far, i, n)
            value = value + down_got[part, cols].astype(jnp.float32)
            down_own[part, cols] = value.astype(jnp.bfloat16)

        pltpu.make_async_copy(down_own.at[part], down_out.at[part], out_sem.at[0, i]).start()
        arrived(up_got.at[part], upr_sem.at[i])

        @pl.loop(0, 2)
        def _(n):
            cols, value = product(x_in, shard, dpre, x_far, 0, dpre_far, i, n)
            value = value + up_got[part, cols].astype(jnp.float32)
            up_own[part, cols] = value.astype(jnp.bfloat16)

        pltpu.make_async_copy(up_own.at[part], up_out.at[part], out_sem.at[1, i]).start()

    for w in range(4):
        arrived(g_send.at[wave_part(w)], gs_sem.at[w])
        arrived(x_send.at[wave_part(w)], rs_sem.at[w])
        arrived(x_far.at[:, span(w)], xfs_sem.at[w])
        arrived(g_far.at[:, span(w)], gfs_sem.at[w])
        arrived(act.at[span(w)], afs_sem.at[w])
        arrived(dpre.at[span(w)], dfs_sem.at[w])
    arrived(terms_a.at[0:1], ts_sem.at[0])
    arrived(terms_b.at[0:1], ts_sem.at[1])
    for i in range(PIECES):
        part = pl.ds(i * step_rows, step_rows)
        arrived(down_send.at[part], dns_sem.at[i])
        arrived(up_send.at[part], ups_sem.at[i])
        pltpu.make_async_copy(down_own.at[part], down_out.at[part], out_sem.at[0, i]).wait()
        pltpu.make_async_copy(up_own.at[part], up_out.at[part], out_sem.at[1, i]).wait()


def on_device(tokens, out_grad, route_slots, expert_counts, router_weight, up_weight, down_weight):
    me = lax.axis_index("expert")
    tok_rows, width = tokens.shape
    hidden = up_weight.shape[2]
    piece = width // 4
    slots = route_slots[0, 0]
    experts, per_slot = slots.shape
    received = experts * per_slot
    with jax.named_scope("gates"):
        order = jnp.stack([shifted(me, step, 1) for step in STEPS])
        slots = slots[order]
        picks = slots[:, :, None] == jnp.arange(tok_rows, dtype=jnp.int32)[None, None, :]
        pick = picks.astype(jnp.bfloat16).reshape(received, tok_rows)
        pick_back = pick.T
        logits = jnp.dot(
            tokens.astype(jnp.float32), router_weight, precision=lax.Precision.HIGHEST
        )
        counts = jnp.maximum(expert_counts, 1).astype(jnp.float32)
        scaled = (jax.nn.sigmoid(logits) / counts[:, None]).T[order]
        weight = jnp.sum(jnp.where(picks, scaled[:, None, :], 0.0), axis=2).reshape(received, 1)
        column = lax.dynamic_slice(router_weight, (0, me), (width, 1)).reshape(1, width)

    half = jnp.bfloat16
    vmem = pl.BlockSpec(memory_space=pltpu.VMEM)
    anywhere = pl.BlockSpec(memory_space=pl.ANY)
    dma = pltpu.SemaphoreType.DMA
    rows_buffer = pltpu.VMEM((received, width), half)
    inner = pltpu.VMEM((received, hidden), half)
    halves = pltpu.VMEM((2, received, piece), half)
    square = pltpu.VMEM((piece, hidden), half)
    full = pltpu.VMEM((width, hidden), half)
    tokens_grad, up_sum, down_sum, terms = pl.pallas_call(
        kernel,
        out_shape=(
            jax.ShapeDtypeStruct((tok_rows, width), half),
            jax.ShapeDtypeStruct((piece, hidden), half),
            jax.ShapeDtypeStruct((piece, hidden), half),
            jax.ShapeDtypeStruct((1, width), jnp.float32),
        ),
        in_specs=[vmem] * 6 + [anywhere] * 2,
        out_specs=(vmem, anywhere, anywhere, vmem),
        scratch_shapes=[
            rows_buffer, rows_buffer, rows_buffer, rows_buffer, rows_buffer, full, full,
            inner, pltpu.VMEM((PER_WAVE * per_slot, hidden), jnp.float32), inner,
            pltpu.VMEM((received, 1), jnp.float32),
            halves, inner, halves, inner, square, square, square, square, square, square,
            pltpu.VMEM((2, width), jnp.float32), pltpu.VMEM((2, width), jnp.float32),
            dma((2,)),
        ]
        + [dma((4,))] * 14
        + [dma((PIECES,))] * 4
        + [dma((2,)), dma((2,)), dma((2, PIECES))],
        compiler_params=pltpu.CompilerParams(
            collective_id=0, has_side_effects=True, vmem_limit_bytes=67043328
        ),
        name="exchange",
    )(tokens, out_grad, pick, pick_back, weight, column, up_weight[0], down_weight[0])
    return (tokens_grad, up_sum[None], down_sum[None], terms.reshape(width, 1))


def solution(mesh):
    return jax.shard_map(
        on_device,
        mesh=mesh,
        in_specs=(
            P(("dp", "expert"), None),
            P(("dp", "expert"), None),
            P("dp", "expert", None, None),
            P(("dp", "expert")),
            P(),
            P("expert", None, None),
            P("expert", None, None),
        ),
        out_specs=(
            P(("dp", "expert"), None),
            P("expert", "dp", None),
            P("expert", "dp", None),
            P(None, "expert"),
        ),
        check_vma=False,
    )
```

time: 320 us -> 224 us (0.70)
  the two profiles are of different devices: /device:TPU:1 before, /device:TPU:6 now
where the time goes in v2:
time: 224 us
  Pallas kernels  208 us (93%)
  local copies, waits for them, and re-layouts  10.5 us (5%)
  matrix products  2.48 us (1%)
  other arithmetic  2.39 us (1%)
    pallas_call x1, Pallas kernels, on_device(): pl.pallas_call(kernel, out_shape=(jax.ShapeDtypeStruct((tok_rows, width),...  208 us
    unnamed x13, local copies, waits for them, and re-layouts  6.79 us

profile of v2, /device:TPU:6, one launch (start us, length us, event | category | flops | bytes accessed | tf_op | source)
XLA Modules:
  0.0 224.1 jit_solution(2823836201524851644)
XLA Ops:
  0.6 0.0 copy-start.3
  0.8 0.1 stack.131
  1.0 0.7 maximum_convert_fusion
  1.6 2.5 %fusion.3 = f32[32,128]{1,0:T(8,128)S(1)} fusion(f32[4096,32]{0,1:T(8,128)} %param.11, bf16[128,4096]{1,0:T(8,128)(2,1)} %tokens.1, f32[128]{0:T(128)S(1)} %maximum_convert_fusion), kind=kOutput, calls=%fused_computation.6 | convolution fusion | flops 201342976 | bytes 1589760 | tf_op jit(solution)/shard_map/gates/dot_general | solution.py:309
  4.1 0.6 gather_fusion.1
  4.7 1.5 dynamic-slice_bitcast_fusion.column
  6.2 0.0 copy-done.3
  6.2 0.1 copy.14
  6.3 0.6 gather_fusion
  6.9 0.2 select_reduce_fusion
  7.1 0.1 eq.190
  7.2 0.7 fusion.5.pick_back
  7.9 0.8 fusion.4.pick
  8.7 0.9 reshape.1267.weight
  9.5 207.9 %exchange.1 = (bf16[128,4096]{1,0:T(8,128)(2,1)}, bf16[1024,1024]{1,0:T(8,128)(2,1)}, bf16[1024,1024]{1,0:T(8,128)(2,1)}, f32[1,4096]{1,0:T(1,128)}) custom-call(bf16[128,4096]{1,0:T(8,128)(2,1)} %tokens.1, bf16[128,4096]{1,0:T(8,128)(2,1)} %grads.1, bf16[512,128]{1,0:T(8,128)(2,1)} %fusion.4.pick, bf16[128,512]{1,0:T(8,128)(2,1)} %fusion.5.pick_back, ...), custom_call_target="tpu_custom_call" | custom-call | tf_op jit(solution)/shard_map/exchange/pallas_call | solution.py:326
  217.4 0.0 copy-start.1
  217.4 2.4 %copy.20 = bf16[128,4096]{1,0:T(8,128)(2,1)} copy(bf16[128,4096]{1,0:T(8,128)(2,1)} %get-tuple-element.16) | data formatting | bytes 2097152
  219.9 0.0 copy-done.1
  219.9 0.0 copy-start
  219.9 1.3 copy.21
  221.2 1.0 copy-done
  222.2 0.0 copy-start.2
  222.2 1.3 copy.22
  223.5 0.0 copy-done.2
  223.5 0.6 copy.23
  (2 shorter events, 0.0 us)
Async XLA Ops:
  0.6 5.6 %copy-start.3 = (s32[1,1,32,16]{2,3,1,0:T(8,128)S(1)}, s32[1,1,32,16]{2,3,1,0:T(8,128)}, u32[]{:S(2)}) copy-start(s32[1,1,32,16]{2,3,1,0:T(8,128)} %param.9) | copy-start | bytes 6148
  217.4 2.4 %copy-start.1 = (bf16[1024,1024]{1,0:T(8,128)(2,1)S(1)}, bf16[1024,1024]{1,0:T(8,128)(2,1)}, u32[]{:S(2)}) copy-start(bf16[1024,1024]{1,0:T(8,128)(2,1)} %get-tuple-element.9) | copy-start | bytes 6291460
  219.9 2.3 %copy-start = (bf16[1024,1024]{1,0:T(8,128)(2,1)S(1)}, bf16[1024,1024]{1,0:T(8,128)(2,1)}, u32[]{:S(2)}) copy-start(bf16[1024,1024]{1,0:T(8,128)(2,1)} %get-tuple-element.10) | copy-start | bytes 6291460
  222.2 1.3 copy-start.2

commit v3 on v2

v3 whole, which is shorter than its diff:
```python
import functools

import jax
import jax.numpy as jnp
from jax import lax
from jax.experimental import pallas as pl
from jax.experimental.pallas import tpu as pltpu
from jax.sharding import PartitionSpec as P

MESH = pl.DeviceIdType.MESH
TRAIL = (((1,), (1,)), ((), ()))
ROWS = (((0,), (0,)), ((), ()))
WAVES = (
    ((1, 1), (3, 3), (1, 3), (3, 1)),
    ((2, 1), (2, 3), (1, 0), (3, 0)),
    ((1, 2), (3, 2), (0, 1), (0, 3)),
    ((0, 0), (2, 2), (2, 0), (0, 2)),
)
STEPS = tuple((dz, dx, dc) for wave in WAVES for dz, dx in wave for dc in (0, 1))
COUNTS = tuple(2 * len(wave) for wave in WAVES)
FIRST = tuple(sum(COUNTS[:w]) for w in range(len(WAVES)))
SELF = STEPS.index((0, 0, 0))
N_WAVES = len(WAVES)
BLOCK = 16
CHUNKS = tuple(
    tuple(range(first, first + count, count if w < N_WAVES - 1 else 2))
    for w, (first, count) in enumerate(zip(FIRST, COUNTS))
)
CHUNK_OF = tuple(
    sum(1 for chunks in CHUNKS for start in chunks if start <= k) - 1 for k in range(len(STEPS))
)
WAVE_OF = tuple(sum(1 for first in FIRST if first <= k) - 1 for k in range(len(STEPS)))
N_CHUNKS = CHUNK_OF[-1] + 1
PIECES = 4


def shifted(me, step, sign):
    dz, dx, dc = step
    z, x, c = me // 8, (me // 2) % 4, me % 2
    other = (c + dc) % 2
    swap = c if sign > 0 else other
    z = (z + sign * (dz + swap * (dx - dz)) + 4) % 4
    x = (x + sign * (dx + swap * (dz - dx)) + 4) % 4
    return (z * 4 + x) * 2 + other


def gelu_pair(values):
    inner = 0.7978845608 * (values + 0.044715 * values * values * values)
    tangent = jnp.tanh(inner)
    result = 0.5 * values * (1.0 + tangent)
    slope = 0.5 * (1.0 + tangent) + 0.5 * values * (1.0 - tangent * tangent) * 0.7978845608 * (
        1.0 + 3.0 * 0.044715 * values * values
    )
    return (result, slope)


def kernel(
    tokens, grads, slots, counts, router, up_hbm, down_hbm,
    tokens_grad, up_out, down_out, terms_out,
    pick, pick_back, scaled, column,
    x_send, g_send, x_in, g_in, r_in, w_up, w_down, act, slope, dpre, logit,
    x_far, dpre_far, g_far, act_far, up_send, down_send, up_got, down_got, own_sum,
    terms_a, terms_b,
    w_sem, xs_sem, xr_sem, gs_sem, gr_sem, rs_sem, rr_sem,
    xfs_sem, xfr_sem, dfs_sem, dfr_sem, gfs_sem, gfr_sem, afs_sem, afr_sem,
    ups_sem, upr_sem, dns_sem, dnr_sem, ts_sem, tr_sem, out_sem,
):
    shard = lax.axis_index("dp")
    me = lax.axis_index("expert")
    mate_a = shard + 1 - 2 * (shard % 2)
    mate_b = 3 - shard
    far = 3 - mate_a
    width = tokens.shape[1]
    hidden = act.shape[1]
    piece = width // 4
    step_rows = piece // PIECES

    load_up = pltpu.make_async_copy(up_hbm, w_up, w_sem.at[0])
    load_down = pltpu.make_async_copy(down_hbm, w_down, w_sem.at[1])
    load_up.start()
    load_down.start()

    barrier = pltpu.get_barrier_semaphore()
    for step in STEPS:
        if step != (0, 0, 0):
            pl.semaphore_signal(
                barrier, inc=1, device_id=(shard, shifted(me, step, 1)), device_id_type=MESH
            )
    pl.semaphore_signal(barrier, inc=1, device_id=(mate_a, me), device_id_type=MESH)
    pl.semaphore_signal(barrier, inc=1, device_id=(mate_b, me), device_id_type=MESH)

    def span(w):
        return pl.ds(FIRST[w] * BLOCK, COUNTS[w] * BLOCK)

    def columns(index, size=piece, offset=0):
        return pl.ds(pl.multiple_of(index * piece + offset, 128), size)

    def arrived(ref, sem):
        pltpu.make_async_copy(ref, ref, sem).wait()

    def remote(src, dst, send, recv, device):
        copy = pltpu.make_async_remote_copy(
            src_ref=src, dst_ref=dst, send_sem=send, recv_sem=recv,
            device_id=device, device_id_type=MESH,
        )
        copy.start()

    def travels(w):
        if FIRST[w] == SELF:
            return pl.ds((SELF + 1) * BLOCK, (COUNTS[w] - 1) * BLOCK)
        return span(w)

    def chunk_rows(start, traveled):
        count = sum(1 for k in CHUNK_OF if k == CHUNK_OF[start])
        skip = 1 if traveled and start == SELF else 0
        return pl.ds((start + skip) * BLOCK, (count - skip) * BLOCK)

    def send_blocks(w, src, dst, send, recv, tags):
        for k in range(FIRST[w], FIRST[w] + COUNTS[w]):
            rows = pl.ds(k * BLOCK, BLOCK)
            if k == SELF:
                dst[rows, :] = src[rows, :]
            else:
                remote(
                    src.at[rows], dst.at[rows], send.at[w], recv.at[tags[k]],
                    (shard, shifted(me, STEPS[k], 1)),
                )

    def return_blocks(w, src, dst, send, recv):
        for k in range(FIRST[w], FIRST[w] + COUNTS[w]):
            rows = pl.ds(k * BLOCK, BLOCK)
            home = pl.ds(pl.multiple_of(me * BLOCK, BLOCK), BLOCK)
            if k == SELF:
                dst[home, :] = src[rows, :]
            else:
                remote(
                    src.at[rows], dst.at[home], send.at[w], recv.at[w],
                    (shard, shifted(me, STEPS[k], -1)),
                )

    def add_terms(w):
        rows = span(w)
        for n in range(8):
            cols = pl.ds(n * 512, 512)
            value = jnp.sum(
                x_in[rows, cols].astype(jnp.float32) * logit[rows, :], axis=0, keepdims=True
            )
            terms_a[0:1, cols] = value if w == 0 else terms_a[0:1, cols] + value

    def wave_steps(w):
        return [shifted(me, STEPS[k], 1) for k in range(FIRST[w], FIRST[w] + COUNTS[w])]

    def wave_picks(w):
        return [pick[pl.ds(pl.multiple_of(to * BLOCK, BLOCK), BLOCK), :] for to in wave_steps(w)]

    def select_tokens(w):
        chosen = jnp.concatenate(wave_picks(w), axis=0)

        @pl.loop(0, 4)
        def _(n):
            cols = columns(n)
            picked = jnp.dot(chosen, tokens[:, cols], preferred_element_type=jnp.float32)
            x_send[span(w), cols] = picked.astype(jnp.bfloat16)

    def select_grads(w):
        picks = wave_picks(w)
        chosen = jnp.concatenate(picks, axis=0)
        weight = jnp.concatenate(
            [
                jnp.sum(one.astype(jnp.float32) * scaled[pl.ds(to, 1), :], axis=1, keepdims=True)
                for one, to in zip(picks, wave_steps(w))
            ],
            axis=0,
        )

        @pl.loop(0, 4)
        def _(n):
            cols = columns(n)
            picked = jnp.dot(chosen, grads[:, cols], preferred_element_type=jnp.float32)
            g_send[span(w), cols] = (weight * picked).astype(jnp.bfloat16)

    tok_rows = tokens.shape[0]
    places = lax.broadcasted_iota(jnp.int32, (tok_rows, slots.shape[1]), 0)
    hits = jnp.where(places == slots[...], 1.0, 0.0)
    pick_back[...] = hits.astype(jnp.bfloat16)
    pick[...] = hits.T.astype(jnp.bfloat16)
    select_tokens(0)
    pl.semaphore_wait(barrier, len(STEPS) + 1)
    send_blocks(0, x_send, x_in, xs_sem, xr_sem, WAVE_OF)

    logits = jnp.zeros((router.shape[0], tok_rows), jnp.float32)
    rest = router[...]
    for _ in range(3):
        head = rest.astype(jnp.bfloat16)
        rest = rest - head.astype(jnp.float32)
        logits = logits + lax.dot_general(
            head, tokens[...], TRAIL, preferred_element_type=jnp.float32
        )
    tallies = jnp.maximum(counts[...], 1).astype(jnp.float32)
    scaled[...] = jax.nn.sigmoid(logits) / tallies
    column[...] = router[pl.ds(me, 1), :]
    for w in range(N_WAVES):
        if w > 0:
            select_tokens(w)
            send_blocks(w, x_send, x_in, xs_sem, xr_sem, WAVE_OF)
        select_grads(w)
        send_blocks(w, g_send, g_in, gs_sem, gr_sem, CHUNK_OF)

    load_up.wait()
    load_down.wait()
    for w in range(N_WAVES):
        rows = span(w)
        wave_rows = COUNTS[w] * BLOCK
        arrived(x_in.at[travels(w)], xr_sem.at[w])
        for slot, index in ((1, far), (0, mate_a)):
            remote(
                x_in.at[rows, columns(index)], x_far.at[slot, rows],
                xfs_sem.at[w], xfr_sem.at[w], (mate_a, me),
            )

        @pl.loop(0, 4)
        def _(n):
            cols = pl.ds(pl.multiple_of(n * 256, 256), 256)
            pre = jnp.dot(x_in[rows, :], w_up[:, cols], preferred_element_type=jnp.float32)
            active, bend = gelu_pair(pre)
            act[rows, cols] = active.astype(jnp.bfloat16)
            slope[0:wave_rows, cols] = bend

        remote(act.at[rows], act_far.at[rows], afs_sem.at[w], afr_sem.at[w], (mate_b, me))
        gate = jnp.zeros((wave_rows, 1), jnp.float32)
        for n in range(4):
            cols = pl.ds(n * piece, piece)
            gate = gate + jnp.sum(
                x_in[rows, cols].astype(jnp.float32) * column[:, cols], axis=1, keepdims=True
            )
        closed = 1.0 - jax.nn.sigmoid(gate)
        for start in CHUNKS[w]:
            tag = CHUNK_OF[start]
            arrived(g_in.at[chunk_rows(start, True)], gr_sem.at[tag])
            some = chunk_rows(start, False)
            for slot, index in ((1, far), (0, mate_b)):
                remote(
                    g_in.at[some, columns(index)], g_far.at[slot, some],
                    gfs_sem.at[tag], gfr_sem.at[tag], (mate_b, me),
                )
        logit[rows, :] = jnp.zeros((wave_rows, 1), jnp.float32)

        @pl.loop(0, 4)
        def _(n):
            cols = pl.ds(pl.multiple_of(n * 256, 256), 256)
            back = jnp.dot(g_in[rows, :], w_down[:, cols], preferred_element_type=jnp.float32)
            logit[rows, :] += jnp.sum(
                act[rows, cols].astype(jnp.float32) * back, axis=1, keepdims=True
            )
            dpre[rows, cols] = (back * slope[0:wave_rows, cols]).astype(jnp.bfloat16)

        remote(dpre.at[rows], dpre_far.at[rows], dfs_sem.at[w], dfr_sem.at[w], (mate_a, me))
        logit[rows, :] = logit[rows, :] * closed
        arrived(x_send.at[travels(w)], xs_sem.at[w])

        @pl.loop(0, 8)
        def _(n):
            cols = pl.ds(pl.multiple_of(n * 512, 512), 512)
            partial = lax.dot_general(
                dpre[rows, :], w_up[cols, :], TRAIL, preferred_element_type=jnp.float32
            )
            partial = partial + logit[rows, :] * column[:, cols]
            x_send[rows, cols] = partial.astype(jnp.bfloat16)

        return_blocks(w, x_send, r_in, rs_sem, rr_sem)
        if w < N_WAVES - 1:
            add_terms(w)

    def product(left, index, right, left_far, slot, right_far, i, n):
        cols = pl.ds(pl.multiple_of(n * 512, 512), 512)
        offset = i * step_rows
        near = lax.dot_general(
            left[:, columns(index, step_rows, offset)], right[:, cols], ROWS,
            preferred_element_type=jnp.float32,
        )
        other = lax.dot_general(
            left_far[slot, :, pl.ds(offset, step_rows)], right_far[:, cols], ROWS,
            preferred_element_type=jnp.float32,
        )
        return cols, near + other

    def up_piece(i):
        part = pl.ds(i * step_rows, step_rows)

        @pl.loop(0, 2)
        def _(n):
            cols, value = product(x_in, mate_b, dpre, x_far, 1, dpre_far, i, n)
            up_send[part, cols] = value.astype(jnp.bfloat16)

        remote(up_send.at[part], up_got.at[part], ups_sem.at[i], upr_sem.at[i], (mate_b, me))

    def down_piece(i):
        part = pl.ds(i * step_rows, step_rows)

        @pl.loop(0, 2)
        def _(n):
            cols, value = product(g_in, mate_a, act, g_far, 1, act_far, i, n)
            down_send[part, cols] = value.astype(jnp.bfloat16)

        remote(down_send.at[part], down_got.at[part], dns_sem.at[i], dnr_sem.at[i], (mate_a, me))

    for chunks in CHUNKS:
        for start in chunks:
            arrived(g_far.at[:, chunk_rows(start, False)], gfr_sem.at[CHUNK_OF[start]])
    for w in range(N_WAVES):
        arrived(act_far.at[span(w)], afr_sem.at[w])
    down_piece(0)
    add_terms(N_WAVES - 1)
    remote(terms_a.at[0:1], terms_a.at[1:2], ts_sem.at[0], tr_sem.at[0], (mate_a, me))
    for w in range(N_WAVES):
        arrived(x_far.at[:, span(w)], xfr_sem.at[w])
        arrived(dpre_far.at[span(w)], dfr_sem.at[w])
    up_piece(0)
    for i in range(1, PIECES):
        down_piece(i)
        up_piece(i)
        if i == 1:
            arrived(terms_a.at[1:2], tr_sem.at[0])
            terms_b[0:1, :] = terms_a[0:1, :] + terms_a[1:2, :]
            remote(terms_b.at[0:1], terms_b.at[1:2], ts_sem.at[1], tr_sem.at[1], (mate_b, me))

    for i in range(PIECES):
        part = pl.ds(i * step_rows, step_rows)

        @pl.loop(0, 2)
        def _(n):
            cols, value = product(g_in, shard, act, g_far, 0, act_far, i, n)
            own_sum[0, :, cols] = value
            cols, value = product(x_in, shard, dpre, x_far, 0, dpre_far, i, n)
            own_sum[1, :, cols] = value

        if i == PIECES - 1:
            arrived(terms_b.at[1:2], tr_sem.at[1])
            terms_out[...] = terms_b[0:1, :] + terms_b[1:2, :]
            for w in range(N_WAVES):
                arrived(r_in.at[travels(w)], rr_sem.at[w])

            @pl.loop(0, 8)
            def _(n):
                cols = pl.ds(pl.multiple_of(n * 512, 512), 512)
                tokens_grad[:, cols] = jnp.dot(
                    pick_back[...], r_in[:, cols], preferred_element_type=jnp.float32
                ).astype(jnp.bfloat16)

        arrived(down_got.at[part], dnr_sem.at[i])
        down_got[part, :] = (own_sum[0] + down_got[part, :].astype(jnp.float32)).astype(
            jnp.bfloat16
        )
        pltpu.make_async_copy(down_got.at[part], down_out.at[part], out_sem.at[0, i]).start()
        arrived(up_got.at[part], upr_sem.at[i])
        up_got[part, :] = (own_sum[1] + up_got[part, :].astype(jnp.float32)).astype(jnp.bfloat16)
        pltpu.make_async_copy(up_got.at[part], up_out.at[part], out_sem.at[1, i]).start()

    for w in range(N_WAVES):
        arrived(g_send.at[travels(w)], gs_sem.at[w])
        arrived(x_send.at[travels(w)], rs_sem.at[w])
        arrived(x_far.at[:, span(w)], xfs_sem.at[w])
        arrived(act.at[span(w)], afs_sem.at[w])
        arrived(dpre.at[span(w)], dfs_sem.at[w])
    for chunks in CHUNKS:
        for start in chunks:
            arrived(g_far.at[:, chunk_rows(start, False)], gfs_sem.at[CHUNK_OF[start]])
    arrived(terms_a.at[0:1], ts_sem.at[0])
    arrived(terms_b.at[0:1], ts_sem.at[1])
    for i in range(PIECES):
        part = pl.ds(i * step_rows, step_rows)
        arrived(down_send.at[part], dns_sem.at[i])
        arrived(up_send.at[part], ups_sem.at[i])
        pltpu.make_async_copy(down_got.at[part], down_out.at[part], out_sem.at[0, i]).wait()
        pltpu.make_async_copy(up_got.at[part], up_out.at[part], out_sem.at[1, i]).wait()


def on_device(tokens, out_grad, route_slots, expert_counts, router_weight, up_weight, down_weight):
    tok_rows, width = tokens.shape
    hidden = up_weight.shape[2]
    piece = width // 4
    slots = route_slots[0, 0]
    experts, per_slot = slots.shape
    received = experts * per_slot
    slots = slots.reshape(1, received)
    counts = expert_counts.reshape(1, tok_rows)
    router = router_weight.T

    half = jnp.bfloat16
    vmem = pl.BlockSpec(memory_space=pltpu.VMEM)
    anywhere = pl.BlockSpec(memory_space=pl.ANY)
    dma = pltpu.SemaphoreType.DMA
    rows_buffer = pltpu.VMEM((received, width), half)
    inner = pltpu.VMEM((received, hidden), half)
    halves = pltpu.VMEM((2, received, piece), half)
    square = pltpu.VMEM((piece, hidden), half)
    full = pltpu.VMEM((width, hidden), half)
    tokens_grad, up_sum, down_sum, terms = pl.pallas_call(
        kernel,
        out_shape=(
            jax.ShapeDtypeStruct((tok_rows, width), half),
            jax.ShapeDtypeStruct((piece, hidden), half),
            jax.ShapeDtypeStruct((piece, hidden), half),
            jax.ShapeDtypeStruct((1, width), jnp.float32),
        ),
        in_specs=[vmem] * 5 + [anywhere] * 2,
        out_specs=(vmem, anywhere, anywhere, vmem),
        scratch_shapes=[
            pltpu.VMEM((received, tok_rows), half), pltpu.VMEM((tok_rows, received), half),
            pltpu.VMEM((experts, tok_rows), jnp.float32), pltpu.VMEM((1, width), jnp.float32),
            rows_buffer, rows_buffer, rows_buffer, rows_buffer, rows_buffer, full, full,
            inner, pltpu.VMEM((max(COUNTS) * BLOCK, hidden), jnp.float32), inner,
            pltpu.VMEM((received, 1), jnp.float32),
            halves, inner, halves, inner, square, square, square, square,
            pltpu.VMEM((2, piece // PIECES, hidden), jnp.float32),
            pltpu.VMEM((2, width), jnp.float32), pltpu.VMEM((2, width), jnp.float32),
            dma((2,)),
        ]
        + [dma((N_WAVES,))] * 3 + [dma((N_CHUNKS,))] + [dma((N_WAVES,))] * 2
        + [dma((N_WAVES,))] * 4 + [dma((N_CHUNKS,))] * 2 + [dma((N_WAVES,))] * 2
        + [dma((PIECES,))] * 4
        + [dma((2,)), dma((2,)), dma((2, PIECES))],
        compiler_params=pltpu.CompilerParams(
            collective_id=0, has_side_effects=True, vmem_limit_bytes=67043328
        ),
        name="exchange",
    )(tokens, out_grad, slots, counts, router, up_weight[0], down_weight[0])
    return (tokens_grad, up_sum[None], down_sum[None], terms.reshape(width, 1))


def solution(mesh):
    return jax.shard_map(
        on_device,
        mesh=mesh,
        in_specs=(
            P(("dp", "expert"), None),
            P(("dp", "expert"), None),
            P("dp", "expert", None, None),
            P(("dp", "expert")),
            P(),
            P("expert", None, None),
            P("expert", None, None),
        ),
        out_specs=(
            P(("dp", "expert"), None),
            P("expert", "dp", None),
            P("expert", "dp", None),
            P(None, "expert"),
        ),
        check_vma=False,
    )
```

time: 224 us -> 199 us (0.89)
  the two profiles are of different devices: /device:TPU:6 before, /device:TPU:1 now
where the time goes in v3:
time: 199 us
  Pallas kernels  190 us (95%)
  local copies, waits for them, and re-layouts  8.15 us (4%)
    pallas_call x1, Pallas kernels, on_device(): pl.pallas_call(kernel, out_shape=(jax.ShapeDtypeStruct((tok_rows, width),...  190 us
    unnamed x11, local copies, waits for them, and re-layouts  7.49 us

profile of v3, /device:TPU:1, one launch (start us, length us, event | category | flops | bytes accessed | tf_op | source)
XLA Modules:
  0.0 198.8 jit_solution(2858903985264579765)
XLA Ops:
  0.6 0.8 copy.12
  1.4 0.7 reshape_squeeze.3.slots
  2.1 190.0 %exchange.1 = (bf16[128,4096]{1,0:T(8,128)(2,1)}, bf16[1024,1024]{1,0:T(8,128)(2,1)}, bf16[1024,1024]{1,0:T(8,128)(2,1)}, f32[1,4096]{1,0:T(1,128)}) custom-call(bf16[128,4096]{1,0:T(8,128)(2,1)} %tokens.1, bf16[128,4096]{1,0:T(8,128)(2,1)} %grads.1, s32[1,512]{1,0:T(1,128)} %reshape_squeeze.3.slots, s32[1,128]{1,0:T(1,128)} %bitcast.15, ...), custom_call_target="tpu_custom_call" | custom-call | tf_op jit(solution)/shard_map/exchange/pallas_call | solution.py:398
  192.1 0.0 copy-start.1
  192.1 2.4 %copy.17 = bf16[128,4096]{1,0:T(8,128)(2,1)} copy(bf16[128,4096]{1,0:T(8,128)(2,1)} %get-tuple-element.16) | data formatting | bytes 2097152
  194.6 0.0 copy-done.1
  194.6 0.0 copy-start
  194.6 1.3 copy.18
  195.9 1.0 copy-done
  196.9 0.0 copy-start.2
  196.9 1.3 copy.19
  198.2 0.0 copy-done.2
  198.2 0.6 copy.20
Async XLA Ops:
  192.1 2.4 %copy-start.1 = (bf16[1024,1024]{1,0:T(8,128)(2,1)S(1)}, bf16[1024,1024]{1,0:T(8,128)(2,1)}, u32[]{:S(2)}) copy-start(bf16[1024,1024]{1,0:T(8,128)(2,1)} %get-tuple-element.9) | copy-start | bytes 6291460
  194.6 2.3 %copy-start = (bf16[1024,1024]{1,0:T(8,128)(2,1)S(1)}, bf16[1024,1024]{1,0:T(8,128)(2,1)}, u32[]{:S(2)}) copy-start(bf16[1024,1024]{1,0:T(8,128)(2,1)} %get-tuple-element.10) | copy-start | bytes 6291460
  196.9 1.3 copy-start.2

commit v4 on v3

--- a/solution.py
+++ b/solution.py
@@ -11,17 +11,23 @@
 TRAIL = (((1,), (1,)), ((), ()))
 ROWS = (((0,), (0,)), ((), ()))
 WAVES = (
+    ((0, 0), (2, 2), (2, 0), (0, 2)),
+    ((2, 1), (2, 3), (0, 1), (0, 3)),
+    ((1, 2), (3, 2), (1, 0), (3, 0)),
     ((1, 1), (3, 3), (1, 3), (3, 1)),
-    ((2, 1), (2, 3), (1, 0), (3, 0)),
-    ((1, 2), (3, 2), (0, 1), (0, 3)),
-    ((0, 0), (2, 2), (2, 0), (0, 2)),
 )
-STEPS = tuple((dz, dx, dc) for wave in WAVES for dz, dx in wave for dc in (0, 1))
+STEPS = tuple(
+    (dz, dx, dc) if dc == 0 else (-dz % 4, -dx % 4, dc)
+    for wave in WAVES
+    for dz, dx in wave
+    for dc in (0, 1)
+)
 COUNTS = tuple(2 * len(wave) for wave in WAVES)
 FIRST = tuple(sum(COUNTS[:w]) for w in range(len(WAVES)))
 SELF = STEPS.index((0, 0, 0))
 N_WAVES = len(WAVES)
 BLOCK = 16
+AHEAD = 2
 CHUNKS = tuple(
     tuple(range(first, first + count, count if w < N_WAVES - 1 else 2))
     for w, (first, count) in enumerate(zip(FIRST, COUNTS))
@@ -147,6 +153,19 @@
             )
             terms_a[0:1, cols] = value if w == 0 else terms_a[0:1, cols] + value
 
+    def give_back(w):
+        rows = span(w)
+        arrived(x_send.at[travels(w)], xs_sem.at[w])
+
+        @pl.loop(0, 8)
+        def _(n):
+            cols = pl.ds(pl.multiple_of(n * 512, 512), 512)
+            partial = lax.dot_general(
+                dpre[rows, :], w_up[cols, :], TRAIL, preferred_element_type=jnp.float32
+            )
+            partial = partial + logit[rows, :] * column[:, cols]
+            x_send[rows, cols] = partial.astype(jnp.bfloat16)
+
     def wave_steps(w):
         return [shifted(me, STEPS[k], 1) for k in range(FIRST[w], FIRST[w] + COUNTS[w])]
 
@@ -199,12 +218,18 @@
     tallies = jnp.maximum(counts[...], 1).astype(jnp.float32)
     scaled[...] = jax.nn.sigmoid(logits) / tallies
     column[...] = router[pl.ds(me, 1), :]
-    for w in range(N_WAVES):
-        if w > 0:
-            select_tokens(w)
-            send_blocks(w, x_send, x_in, xs_sem, xr_sem, WAVE_OF)
+    def send_tokens(w):
+        select_tokens(w)
+        send_blocks(w, x_send, x_in, xs_sem, xr_sem, WAVE_OF)
+
+    def send_grads(w):
         select_grads(w)
         send_blocks(w, g_send, g_in, gs_sem, gr_sem, CHUNK_OF)
+
+    send_grads(0)
+    for w in range(1, AHEAD):
+        send_tokens(w)
+        send_grads(w)
 
     load_up.wait()
     load_down.wait()
@@ -212,6 +237,8 @@
         rows = span(w)
         wave_rows = COUNTS[w] * BLOCK
         arrived(x_in.at[travels(w)], xr_sem.at[w])
+        if w + AHEAD < N_WAVES:
+            send_tokens(w + AHEAD)
         for slot, index in ((1, far), (0, mate_a)):
             remote(
                 x_in.at[rows, columns(index)], x_far.at[slot, rows],
@@ -243,6 +270,11 @@
                     g_in.at[some, columns(index)], g_far.at[slot, some],
                     gfs_sem.at[tag], gfr_sem.at[tag], (mate_b, me),
                 )
+        if w + AHEAD < N_WAVES:
+            send_grads(w + AHEAD)
+            if w + AHEAD == N_WAVES - 1:
+                for early in range(w):
+                    return_blocks(early, x_send, r_in, rs_sem, rr_sem)
         logit[rows, :] = jnp.zeros((wave_rows, 1), jnp.float32)
 
         @pl.loop(0, 4)
@@ -256,18 +288,9 @@
 
         remote(dpre.at[rows], dpre_far.at[rows], dfs_sem.at[w], dfr_sem.at[w], (mate_a, me))
         logit[rows, :] = logit[rows, :] * closed
-        arrived(x_send.at[travels(w)], xs_sem.at[w])
-
-        @pl.loop(0, 8)
-        def _(n):
-            cols = pl.ds(pl.multiple_of(n * 512, 512), 512)
-            partial = lax.dot_general(
-                dpre[rows, :], w_up[cols, :], TRAIL, preferred_element_type=jnp.float32
-            )
-            partial = partial + logit[rows, :] * column[:, cols]
-            x_send[rows, cols] = partial.astype(jnp.bfloat16)
-
-        return_blocks(w, x_send, r_in, rs_sem, rr_sem)
+        give_back(w)
+        if w + AHEAD >= N_WAVES - 1:
+            return_blocks(w, x_send, r_in, rs_sem, rr_sem)
         if w < N_WAVES - 1:
             add_terms(w)
 

time: 199 us -> 187 us (0.940)
  Pallas kernels: 190 us -> 178 us
    pallas_call x1, Pallas kernels: 190 us -> 178 us  [on_device(): pl.pallas_call(kernel, out_shape=(jax.ShapeDtypeStruct((tok_rows, width),...]
where the time goes in v4:
time: 187 us
  Pallas kernels  178 us (95%)
  local copies, waits for them, and re-layouts  8.15 us (4%)
    pallas_call x1, Pallas kernels, on_device(): pl.pallas_call(kernel, out_shape=(jax.ShapeDtypeStruct((tok_rows, width),...  178 us
    unnamed x11, local copies, waits for them, and re-layouts  7.49 us

profile of v4, /device:TPU:1, one launch (start us, length us, event | category | flops | bytes accessed | tf_op | source)
XLA Modules:
  0.0 186.6 jit_solution(12521895561422128864)
XLA Ops:
  0.6 0.8 copy.12
  1.4 0.7 reshape_squeeze.3.slots
  2.1 177.8 %exchange.1 = (bf16[128,4096]{1,0:T(8,128)(2,1)}, bf16[1024,1024]{1,0:T(8,128)(2,1)}, bf16[1024,1024]{1,0:T(8,128)(2,1)}, f32[1,4096]{1,0:T(1,128)}) custom-call(bf16[128,4096]{1,0:T(8,128)(2,1)} %tokens.1, bf16[128,4096]{1,0:T(8,128)(2,1)} %grads.1, s32[1,512]{1,0:T(1,128)} %reshape_squeeze.3.slots, s32[1,128]{1,0:T(1,128)} %bitcast.15, ...), custom_call_target="tpu_custom_call" | custom-call | tf_op jit(solution)/shard_map/exchange/pallas_call | solution.py:421
  179.9 0.0 copy-start.1
  179.9 2.4 %copy.17 = bf16[128,4096]{1,0:T(8,128)(2,1)} copy(bf16[128,4096]{1,0:T(8,128)(2,1)} %get-tuple-element.16) | data formatting | bytes 2097152
  182.3 0.0 copy-done.1
  182.3 0.0 copy-start
  182.3 1.3 copy.18
  183.7 1.0 copy-done
  184.7 0.0 copy-start.2
  184.7 1.3 copy.19
  186.0 0.0 copy-done.2
  186.0 0.6 copy.20
Async XLA Ops:
  179.9 2.4 %copy-start.1 = (bf16[1024,1024]{1,0:T(8,128)(2,1)S(1)}, bf16[1024,1024]{1,0:T(8,128)(2,1)}, u32[]{:S(2)}) copy-start(bf16[1024,1024]{1,0:T(8,128)(2,1)} %get-tuple-element.9) | copy-start | bytes 6291460
  182.3 2.3 %copy-start = (bf16[1024,1024]{1,0:T(8,128)(2,1)S(1)}, bf16[1024,1024]{1,0:T(8,128)(2,1)}, u32[]{:S(2)}) copy-start(bf16[1024,1024]{1,0:T(8,128)(2,1)} %get-tuple-element.10) | copy-start | bytes 6291460
  184.7 1.3 copy-start.2

commit v5 on v4

--- a/solution.py
+++ b/solution.py
@@ -29,7 +29,7 @@
 BLOCK = 16
 AHEAD = 2
 CHUNKS = tuple(
-    tuple(range(first, first + count, count if w < N_WAVES - 1 else 2))
+    tuple(range(first, first + count, count if w < N_WAVES - 1 else count // 2))
     for w, (first, count) in enumerate(zip(FIRST, COUNTS))
 )
 CHUNK_OF = tuple(
@@ -396,6 +396,27 @@
         arrived(up_send.at[part], ups_sem.at[i])
         pltpu.make_async_copy(down_got.at[part], down_out.at[part], out_sem.at[0, i]).wait()
         pltpu.make_async_copy(up_got.at[part], up_out.at[part], out_sem.at[1, i]).wait()
+
+
+def hand_over(first, second, third, first_out, second_out, third_out, a, b, c, in_sem, sem):
+    moves = []
+    for n, (src, mid, dst) in enumerate(
+        ((first, a, first_out), (second, b, second_out), (third, c, third_out))
+    ):
+        rows = src.shape[0] // 4
+        for i in range(4):
+            part = pl.ds(i * rows, rows)
+            load = pltpu.make_async_copy(src.at[part], mid.at[part], in_sem.at[n, i])
+            load.start()
+            moves.append((load, mid.at[part], dst.at[part], sem.at[n, i]))
+    stores = []
+    for load, mid, dst, one in moves:
+        load.wait()
+        store = pltpu.make_async_copy(mid, dst, one)
+        store.start()
+        stores.append(store)
+    for store in stores:
+        store.wait()
 
 
 def on_device(tokens, out_grad, route_slots, expert_counts, router_weight, up_weight, down_weight):
@@ -448,6 +469,16 @@
         ),
         name="exchange",
     )(tokens, out_grad, slots, counts, router, up_weight[0], down_weight[0])
+    results = (tokens_grad, up_sum, down_sum)
+    tokens_grad, up_sum, down_sum = pl.pallas_call(
+        hand_over,
+        out_shape=tuple(jax.ShapeDtypeStruct(one.shape, one.dtype) for one in results),
+        in_specs=[anywhere] * 3,
+        out_specs=(anywhere,) * 3,
+        scratch_shapes=[pltpu.VMEM(one.shape, one.dtype) for one in results]
+        + [dma((3, 4)), dma((3, 4))],
+        name="hand_over",
+    )(*results)
     return (tokens_grad, up_sum[None], down_sum[None], terms.reshape(width, 1))
 
 

time: 187 us -> 185 us (0.989); the launches traced: 187 us -> 182 us
  local copies, waits for them, and re-layouts: 8.15 us -> 2.05 us
  Pallas kernels: 178 us -> 180 us
    unnamed x11 -> x4, local copies, waits for them, and re-layouts: 7.49 us -> 1.38 us
    pallas_call x0 -> x1, Pallas kernels: none -> 4.8 us  [on_device(): pl.pallas_call(hand_over, out_shape=tuple((jax.ShapeDtypeStruct(one.shape...]
    pallas_call x1, Pallas kernels: 178 us -> 175 us  [on_device(): pl.pallas_call(kernel, out_shape=(jax.ShapeDtypeStruct((tok_rows, width),...]
where the time goes in v5:
time: 185 us; the launch traced here: 182 us
  Pallas kernels  180 us (97%)
  local copies, waits for them, and re-layouts  2.05 us (1%)
    pallas_call x1, Pallas kernels, on_device(): pl.pallas_call(kernel, out_shape=(jax.ShapeDtypeStruct((tok_rows, width),...  175 us
    pallas_call x1, Pallas kernels, on_device(): pl.pallas_call(hand_over, out_shape=tuple((jax.ShapeDtypeStruct(one.shape...  4.8 us

profile of v5, /device:TPU:1, one launch (start us, length us, event | category | flops | bytes accessed | tf_op | source)
XLA Modules:
  0.0 182.3 jit_solution(15928417557210380859)
XLA Ops:
  0.6 0.8 copy.12
  1.4 0.7 reshape_squeeze.3.slots
  2.1 174.8 %exchange.1 = (bf16[128,4096]{1,0:T(8,128)(2,1)}, bf16[1024,1024]{1,0:T(8,128)(2,1)}, bf16[1024,1024]{1,0:T(8,128)(2,1)}, f32[1,4096]{1,0:T(1,128)}) custom-call(bf16[128,4096]{1,0:T(8,128)(2,1)} %tokens.1, bf16[128,4096]{1,0:T(8,128)(2,1)} %grads.1, s32[1,512]{1,0:T(1,128)} %reshape_squeeze.3.slots, s32[1,128]{1,0:T(1,128)} %bitcast.13, ...), custom_call_target="tpu_custom_call" | custom-call | tf_op jit(solution)/shard_map/exchange/pallas_call | solution.py:442
  176.9 0.0 copy-start
  176.9 4.8 %hand_over.1 = (bf16[128,4096]{1,0:T(8,128)(2,1)}, bf16[1024,1024]{1,0:T(8,128)(2,1)}, bf16[1024,1024]{1,0:T(8,128)(2,1)}) custom-call(bf16[128,4096]{1,0:T(8,128)(2,1)} %get-tuple-element.11.first, bf16[1024,1024]{1,0:T(8,128)(2,1)} %get-tuple-element.12.second, bf16[1024,1024]{1,0:T(8,128)(2,1)} %get-tuple-element.13.third), custom_call_target="tpu_custom_call" | custom-call | tf_op jit(solution)/shard_map/hand_over/pallas_call | solution.py:473
  181.7 0.0 copy-done
  181.7 0.6 copy.14
Async XLA Ops:
  176.9 4.8 %copy-start = (f32[1,4096]{1,0:T(1,128)S(1)}, f32[1,4096]{1,0:T(1,128)}, u32[]{:S(2)}) copy-start(f32[1,4096]{1,0:T(1,128)} %get-tuple-element.17) | copy-start | bytes 49156

commit v6 on v5

--- a/solution.py
+++ b/solution.py
@@ -37,7 +37,7 @@
 )
 WAVE_OF = tuple(sum(1 for first in FIRST if first <= k) - 1 for k in range(len(STEPS)))
 N_CHUNKS = CHUNK_OF[-1] + 1
-PIECES = 4
+PIECES = 8
 
 
 def shifted(me, step, sign):

time: 185 us -> 184 us (level)
  no operation moved by 1% of the time
where the time goes in v6:
time: 184 us; the launch traced here: 182 us
  Pallas kernels  179 us (97%)
  local copies, waits for them, and re-layouts  2.05 us (1%)
    pallas_call x1, Pallas kernels, on_device(): pl.pallas_call(kernel, out_shape=(jax.ShapeDtypeStruct((tok_rows, width),...  175 us
    pallas_call x1, Pallas kernels, on_device(): pl.pallas_call(hand_over, out_shape=tuple((jax.ShapeDtypeStruct(one.shape...  4.8 us

profile of v6, /device:TPU:1, one launch (start us, length us, event | category | flops | bytes accessed | tf_op | source)
XLA Modules:
  0.0 182.1 jit_solution(2182703857373896146)
XLA Ops:
  0.6 0.8 copy.12
  1.4 0.7 reshape_squeeze.3.slots
  2.1 174.6 %exchange.1 = (bf16[128,4096]{1,0:T(8,128)(2,1)}, bf16[1024,1024]{1,0:T(8,128)(2,1)}, bf16[1024,1024]{1,0:T(8,128)(2,1)}, f32[1,4096]{1,0:T(1,128)}) custom-call(bf16[128,4096]{1,0:T(8,128)(2,1)} %tokens.1, bf16[128,4096]{1,0:T(8,128)(2,1)} %grads.1, s32[1,512]{1,0:T(1,128)} %reshape_squeeze.3.slots, s32[1,128]{1,0:T(1,128)} %bitcast.13, ...), custom_call_target="tpu_custom_call" | custom-call | tf_op jit(solution)/shard_map/exchange/pallas_call | solution.py:442
  176.6 0.0 copy-start
  176.6 4.8 %hand_over.1 = (bf16[128,4096]{1,0:T(8,128)(2,1)}, bf16[1024,1024]{1,0:T(8,128)(2,1)}, bf16[1024,1024]{1,0:T(8,128)(2,1)}) custom-call(bf16[128,4096]{1,0:T(8,128)(2,1)} %get-tuple-element.11.first, bf16[1024,1024]{1,0:T(8,128)(2,1)} %get-tuple-element.12.second, bf16[1024,1024]{1,0:T(8,128)(2,1)} %get-tuple-element.13.third), custom_call_target="tpu_custom_call" | custom-call | tf_op jit(solution)/shard_map/hand_over/pallas_call | solution.py:473
  181.4 0.0 copy-done
  181.5 0.6 copy.14
Async XLA Ops:
  176.6 4.8 %copy-start = (f32[1,4096]{1,0:T(1,128)S(1)}, f32[1,4096]{1,0:T(1,128)}, u32[]{:S(2)}) copy-start(f32[1,4096]{1,0:T(1,128)} %get-tuple-element.17) | copy-start | bytes 49156
